TPU v7x, 32 devices: a whole 2x2x4 slice. The times are simulated.
32 devices in a mesh: groups: 2 (over y), seq: 4 (over z), head: 2 (over x), sub: 2 (over core).
Axes of the slice: x: 2, y: 2, z: 4, core: 2. Of those that a mesh axis runs over, the one named last changes fastest.
Arguments:
- tokens: bfloat16 [4096, 3072], P(('groups', 'seq')), parts along dimension 0, may hold values from -6 to 6
- modulation: float32 [3, 3072], replicated, may hold values from -4 to 4
- w_qkv: bfloat16 [3072, 8, 768], P('seq', ('head', 'sub')), may hold values from -0.15625 to 0.15625
- w_out: bfloat16 [2048, 3072], P('seq', ('head', 'sub')), may hold values from -0.125 to 0.125
- pattern: int32 [32, 4], P(('groups', 'seq')), parts along dimension 0, may hold values from 0 to 15, as said below
- counts: int32 [32], P(('groups', 'seq')), parts along dimension 0, may hold values from 1 to 4, as said below
- spatial_mask: int32 [8, 4, 4], P(('groups', 'seq')), parts along dimension 0, may hold values from 0 to 1, as said below
Outputs:
- update: bfloat16 [4096, 3072], P(('groups', 'seq'), ('head', 'sub')), parts along dimension 0
There are 2 independent parts, one for each index of `groups`. A program takes and returns all parts, laid end to end along the dimension named above; an argument that names none is the same for every part. Nothing has to cross between parts.
Inputs may be any that keep to these rules, and one draw needn't show every extreme that they name: pattern[b, 0] = b; each further entry of row b is b plus a nonzero offset of size at most 2, the offsets of one row different, clipped to the blocks of the video. `counts`: blocks with a count above one all lie in one cyclic run of half of the 16 blocks. `spatial_mask`: every diagonal entry is 1.
All inputs are finite; a program needn't handle non-finite values.
Results may differ from a plain program's by a relative error of at most 0.012.
The roundings to bfloat16 on the way count: a program that leaves them out, or rounds other values in their place, can miss the bound.
Values may be sent and summed in bfloat16 or wider, within the bound.
A program may use at most 128 MiB of HBM per device.

v0:
```python
import math

import jax
import jax.numpy as jnp
from jax import lax
from jax.sharding import PartitionSpec as P

BLOCK = 128
WIN = 2


EPSILON = 1e-06


def with_halo(cells, sides, width):
    for axis, dim in sides:
        count = lax.axis_size(axis)
        ends = count - 1
        head = lax.slice_in_dim(cells, 0, width, axis=dim)
        tail = lax.slice_in_dim(cells, cells.shape[dim] - width, cells.shape[dim], axis=dim)
        cells = jnp.concatenate(
            [
                lax.ppermute(tail, axis, [(i, (i + 1) % count) for i in range(ends)]),
                cells,
                lax.ppermute(head, axis, [((i + 1) % count, i) for i in range(ends)]),
            ],
            axis=dim,
        )
    return cells


def modulate(tokens, modulation):
    values = tokens.astype(jnp.float32)
    center = jnp.mean(values, axis=-1, keepdims=True)
    spread = jnp.mean(jnp.square(values - center), axis=-1, keepdims=True)
    normed = (values - center) * lax.rsqrt(spread + EPSILON)
    return (normed * (1.0 + modulation[1]) + modulation[0]).astype(jnp.bfloat16)


def shards(tokens, modulation, w_qkv, w_out, pattern, counts, spatial_mask):
    row_count, feature_width = tokens.shape
    pairs_local = w_qkv.shape[1]
    head_size = w_qkv.shape[2] // 6
    frames_local = spatial_mask.shape[0]
    positions = row_count // frames_local
    slot_total = pattern.shape[1]
    scale_factor = 1.0 / math.sqrt(head_size)
    hidden = modulate(tokens, modulation)
    piece = lax.all_gather(w_qkv, "seq", axis=0, tiled=True)
    projected = jnp.dot(
        hidden, piece.reshape(piece.shape[0], -1), preferred_element_type=jnp.float32
    )
    whole_out = lax.all_gather(w_out, "seq", axis=0, tiled=True)
    packed = projected.astype(jnp.bfloat16).reshape(
        frames_local, positions, pairs_local, 6 * head_size
    )
    temporal_in = packed[..., : 3 * head_size].transpose(1, 0, 2, 3)
    received = lax.all_to_all(temporal_in, "seq", split_axis=0, concat_axis=1, tiled=True)
    position_span, frame_total, items, _ = received.shape
    relaid = received.reshape(position_span * frame_total, items, 3 * head_size)
    extended = with_halo(relaid[:, :, head_size:], (("seq", 0),), WIN * BLOCK)
    block_count = position_span * frame_total // BLOCK
    key_table = extended.reshape(block_count + 2 * WIN, BLOCK, items, 2 * head_size)
    queries = relaid[:, :, :head_size].reshape(block_count, BLOCK, items, head_size)
    offsets = pattern - (lax.axis_index("seq") * block_count - WIN)

    def slot_step(slot_index, state_pair):
        numerator, denominator = state_pair
        chosen = lax.dynamic_index_in_dim(offsets, slot_index, 1, keepdims=False)
        picked = jnp.take(key_table, chosen, axis=0)
        scores = (
            jnp.einsum(
                "bqnc,bknc->bnqk",
                queries,
                picked[..., :head_size],
                preferred_element_type=jnp.float32,
            )
            * scale_factor
        )
        alive = (slot_index < counts).astype(jnp.float32)
        weights = jnp.exp(scores) * alive[:, None, None, None]
        numerator = numerator + jnp.einsum(
            "bnqk,bknc->bnqc",
            weights.astype(jnp.bfloat16),
            picked[..., head_size:],
            preferred_element_type=jnp.float32,
        )
        return (numerator, denominator + jnp.sum(weights, axis=-1))

    start_state = (
        jnp.zeros((block_count, items, BLOCK, head_size), jnp.float32),
        jnp.zeros((block_count, items, BLOCK), jnp.float32),
    )
    numerator, denominator = lax.fori_loop(0, slot_total, slot_step, start_state)
    outcome = (numerator / denominator[..., None]).astype(jnp.bfloat16)
    outcome = outcome.transpose(0, 2, 1, 3).reshape(position_span, frame_total, items, head_size)
    temporal_out = lax.all_to_all(outcome, "seq", split_axis=1, concat_axis=0, tiled=True)
    spatial = packed[..., 3 * head_size :]
    blocks_frame = positions // BLOCK
    scores = (
        jnp.einsum(
            "fpnc,fqnc->fnpq",
            spatial[..., :head_size],
            spatial[..., head_size : 2 * head_size],
            preferred_element_type=jnp.float32,
        )
        * scale_factor
    )
    keep = spatial_mask.astype(jnp.float32)[:, None, :, None, :, None]
    weights = (
        jnp.exp(scores).reshape(frames_local, pairs_local, blocks_frame, BLOCK, blocks_frame, BLOCK)
        * keep
    )
    weights = weights.reshape(frames_local, pairs_local, positions, positions)
    denominator = jnp.sum(weights, axis=-1)
    numerator = jnp.einsum(
        "fnpq,fqnc->fpnc",
        weights.astype(jnp.bfloat16),
        spatial[..., 2 * head_size :],
        preferred_element_type=jnp.float32,
    )
    spatial_out = (numerator / denominator.transpose(0, 2, 1)[..., None]).astype(jnp.bfloat16)
    attention = jnp.concatenate([temporal_out.transpose(1, 0, 2, 3), spatial_out], axis=-1)
    attention = attention.reshape(row_count, pairs_local, 2 * head_size)
    out_width = whole_out.shape[1]
    mixed = jnp.dot(
        lax.all_gather(attention, ("head", "sub"), axis=1, tiled=True).reshape(row_count, -1),
        whole_out,
        preferred_element_type=jnp.float32,
    )
    gate_slice = lax.dynamic_slice_in_dim(
        modulation[2], lax.axis_index(("head", "sub")) * out_width, out_width, 0
    )
    return (gate_slice * mixed).astype(jnp.bfloat16)


def solution(mesh):
    return jax.shard_map(
        shards,
        mesh=mesh,
        in_specs=(
            P(("groups", "seq"), None),
            P(),
            P("seq", ("head", "sub"), None),
            P("seq", ("head", "sub")),
            P(("groups", "seq"), None),
            P(("groups", "seq")),
            P(("groups", "seq"), None, None),
        ),
        out_specs=P(("groups", "seq"), ("head", "sub")),
        check_vma=False,
    )
```

profile of v0, /device:TPU:25, one launch (start us, length us, event | category | flops | bytes accessed | tf_op | source)
XLA Modules:
  0.0 356.3 jit_solution(18314034296797499365)
XLA Ops:
  6.5 0.7 all-gather.5.cloned.1.call-update
  7.3 2.6 convert_reduce_fusion
  9.9 1.0 fusion.8
  10.9 162.9 %all-gather.5.cloned.1.call-done = bf16[3072,2,768]{2,1,0:T(2,128)(2,1)} async-done(((bf16[768,2,768]{2,1,0:T(2,128)(2,1)}), bf16[3072,2,768]{2,1,0:T(2,128)(2,1)}) %all-gather.5.cloned.1.call-update) | async-done | bytes 9437200 | tf_op jit(solution)/shard_map/all_gather | solution.py:49
  173.8 9.0 %copy.65 = bf16[384,8,2,768]{3,1,2,0:T(8,128)(2,1)} copy(bf16[384,8,2,768]{3,2,1,0:T(2,128)(2,1)} %bitcast.76) | data formatting | bytes 18874368
  182.8 10.0 %fusion.18 = bf16[512,1536]{1,0:T(8,128)(2,1)} fusion(bf16[3072,1536]{1,0:T(8,128)(2,1)} %bitcast.77, bf16[512,3072]{1,0:T(8,128)(2,1)S(1)} %copy-done, f32[3072]{0:T(1024)S(1)} %bitcast.89, f32[3072]{0:T(1024)S(1)} %bitcast.90, f32[512]{0:T(512)S(1)} %add_rsqrt_fusion, f32[512]{0:T(512)S(1)} %broadcast_multiply_fusion), kind=kOutput, calls=%fused_computation.28 | convolution fusion | flops 4842061824 | bytes 14184448 | tf_op jit(solution)/shard_map/dot_general | solution.py:50
  192.8 3.6 %reshape.85 = bf16[1,512,2,768]{3,2,1,0:T(2,128)(2,1)S(1)} reshape(bf16[512,1536]{1,0:T(8,128)(2,1)} %fusion.18) | data formatting | bytes 3145728 | tf_op jit(solution)/shard_map/reshape | solution.py:54
  196.4 1.4 slice_bitcast_fusion
  197.9 6.7 %all-to-all-start = ((bf16[512,1,2,384]{3,2,1,0:T(2,128)(2,1)}), bf16[512,1,2,384]{3,2,1,0:T(2,128)(2,1)S(1)}, u32[]{:S(2)}, u32[]{:S(2)}) async-start(bf16[512,1,2,384]{3,2,1,0:T(2,128)(2,1)} %slice_bitcast_fusion), calls=%async_computation | async-start | bytes 1572864 | tf_op jit(solution)/shard_map/all_to_all | solution.py:58
  204.7 17.5 %all-to-all-done = bf16[512,1,2,384]{3,2,1,0:T(2,128)(2,1)S(1)} async-done(((bf16[512,1,2,384]{3,2,1,0:T(2,128)(2,1)}), bf16[512,1,2,384]{3,2,1,0:T(2,128)(2,1)S(1)}, u32[]{:S(2)}, u32[]{:S(2)}) %all-to-all-start) | async-done | bytes 786464 | tf_op jit(solution)/shard_map/all_to_all | solution.py:58
  222.2 1.5 copy.81
  223.7 1.6 reshape.86
  225.3 0.9 fusion.34
  226.2 1.3 collective-permute-start
  227.4 4.7 %collective-permute-start.1 = (bf16[256,2,256]{2,0,1:T(8,128)(2,1)}, bf16[256,2,256]{2,0,1:T(8,128)(2,1)}, u32[]{:S(2)}, u32[]{:S(2)}) collective-permute-start(bf16[256,2,256]{2,0,1:T(8,128)(2,1)} %get-tuple-element.199), channel_id=1, source_target_pairs={{4,0},{8,4},{12,8},{5,1},{9,5},{13,9},{6,2},{10,6},{14,10},{7,3},{... | collective-permute-start | bytes 786440 | tf_op jit(solution)/shard_map/ppermute | solution.py:25
  232.3 0.2 mul.111
  232.5 1.1 copy.80
  233.5 1.2 fusion.33
  234.9 0.9 collective-permute-done.1
  235.8 1.1 pad_maximum_fusion
  237.0 5.9 %while.16 = (s32[]{:T(128)}, f32[4,2,128,128]{3,2,1,0:T(8,128)S(1)}, f32[4,2,128]{2,1,0:T(2,128)S(1)}, s32[4,4]{0,1:T(4,128)S(1)}, bf16[8,128,2,256]{3,1,2,0:T(8...) while((s32[]{:T(128)}, ...), condition=%wide.region_4.5_spmd.clone, body=%wide.region_2.4_spmd.clone.sunk | while | flops 68159520 | bytes 4477664 | solution.py:94
  237.0 0.6 gather_fusion
  237.6 0.1 broadcast_select_fusion.2
  237.7 0.3 fusion.48
  238.1 0.3 convolution_add_fusion.2
  238.5 0.6 gather_fusion
  239.2 0.3 fusion.48
  239.6 0.3 convolution_add_fusion.2
  240.0 0.6 gather_fusion
  240.7 0.3 fusion.48
  241.1 0.3 convolution_add_fusion.2
  241.5 0.6 gather_fusion
  242.2 0.3 fusion.48
  242.5 0.3 convolution_add_fusion.2
  242.9 0.2 fusion.28
  243.2 0.8 copy.51
  243.9 6.6 %all-to-all-start.1 = ((bf16[128,4,2,128]{3,0,2,1:T(8,128)(2,1)}), bf16[128,4,2,128]{3,0,2,1:T(8,128)(2,1)S(1)}, u32[]{:S(2)}, u32[]{:S(2)}) async-start(bf16[128,4,2,128]{3,0,2,1:T(8,128)(2,1)} %copy.51), calls=%async_computation.1 | async-start | bytes 524288 | tf_op jit(solution)/shard_map/all_to_all | solution.py:97
  250.5 1.9 fusion.21
  252.4 0.2 copy.62
  252.5 2.1 fusion.24
  254.7 1.6 all-to-all-done.1
  256.3 0.2 copy.52
  256.7 1.0 copy.58
  257.7 0.7 all-gather.7.cloned.1.call-update
  258.5 24.5 %all-gather.9.cloned.1.call-done = bf16[1,512,8,256]{3,1,0,2:T(8,128)(2,1)} async-done(((bf16[1,512,2,256]{3,1,0,2:T(8,128)(2,1)}), bf16[1,512,8,256]{3,1,0,2:T(8,128)(2,1)}) %all-gather.9.cloned.1.call-update) | async-done | bytes 2097168 | tf_op jit(solution)/shard_map/all_gather | solution.py:127
  282.9 2.9 copy.59
  285.8 59.4 %all-gather.7.cloned.1.call-done = bf16[2048,768]{1,0:T(8,128)(2,1)} async-done(((bf16[512,768]{1,0:T(8,128)(2,1)}), bf16[2048,768]{1,0:T(8,128)(2,1)}) %all-gather.7.cloned.1.call-update) | async-done | bytes 3145744 | tf_op jit(solution)/shard_map/all_gather | solution.py:53
  345.2 4.6 %multiply_convert_fusion = bf16[512,768]{1,0:T(8,128)(2,1)} fusion(bf16[512,2048]{0,1:T(8,128)(2,1)S(1)} %bitcast.84, bf16[2048,768]{1,0:T(8,128)(2,1)} %all-gather.7.cloned.1.call-done, f32[768]{0:T(1024)S(1)} %dynamic-slice_reduce_fusion), kind=kOutput, calls=%fused_computation.32 | convolution fusion | flops 1611399168 | bytes 6032384 | tf_op jit(solution)/shard_map/dot_general | solution.py:126
  (55 shorter events, 1.2 us)
Async XLA Ops:
  6.5 167.2 %all-gather.5.cloned.1.call-start = ((), (), s32[]{:S(2)}) async-start(), calls=%async_computation.2 | async-start | bytes 11796480 | tf_op jit(solution)/shard_map/all_gather | solution.py:49
  6.5 3.3 copy-start
  9.9 1.0 copy-start.3
  196.4 8.2 %copy-start.4 = (s32[4,4]{1,0:T(4,128)S(1)}, s32[4,4]{1,0:T(4,128)}, u32[]{:S(2)}) copy-start(s32[4,4]{1,0:T(4,128)} %param.13) | copy-start | bytes 196
  196.4 8.3 %copy-start.5 = (s32[1,4,4]{2,1,0:T(4,128)S(1)}, s32[1,4,4]{2,1,0:T(4,128)}, u32[]{:S(2)}) copy-start(s32[1,4,4]{2,1,0:T(4,128)} %param.15) | copy-start | bytes 196
  197.9 24.4 %all-to-all-start = ((bf16[512,1,2,384]{3,2,1,0:T(2,128)(2,1)}), bf16[512,1,2,384]{3,2,1,0:T(2,128)(2,1)S(1)}, u32[]{:S(2)}, u32[]{:S(2)}) async-start(bf16[512,1,2,384]{3,2,1,0:T(2,128)(2,1)} %slice_bitcast_fusion), calls=%async_computation | async-start | bytes 1572864 | tf_op jit(solution)/shard_map/all_to_all | solution.py:58
  226.2 8.7 %collective-permute-start = (bf16[256,2,256]{2,0,1:T(8,128)(2,1)}, bf16[256,2,256]{2,0,1:T(8,128)(2,1)}, u32[]{:S(2)}, u32[]{:S(2)}) collective-permute-start(bf16[256,2,256]{2,0,1:T(8,128)(2,1)} %get-tuple-element.198), channel_id=1, source_target_pairs={{0,4},{4,8},{8,12},{1,5},{5,9},{9,13},{2,6},{6,10},{10,14},{3,7},{... | collective-permute-start | bytes 786440 | tf_op jit(solution)/shard_map/ppermute | solution.py:23
  227.4 8.3 %collective-permute-start.1 = (bf16[256,2,256]{2,0,1:T(8,128)(2,1)}, bf16[256,2,256]{2,0,1:T(8,128)(2,1)}, u32[]{:S(2)}, u32[]{:S(2)}) collective-permute-start(bf16[256,2,256]{2,0,1:T(8,128)(2,1)} %get-tuple-element.199), channel_id=1, source_target_pairs={{4,0},{8,4},{12,8},{5,1},{9,5},{13,9},{6,2},{10,6},{14,10},{7,3},{... | collective-permute-start | bytes 786440 | tf_op jit(solution)/shard_map/ppermute | solution.py:25
  234.8 2.1 copy-start.6
  242.9 7.6 %copy-start.1 = (f32[64,8,4,128]{3,1,2,0:T(8,128)S(1)}, f32[64,8,4,128]{3,1,2,0:T(8,128)}, u32[]{:S(2)}) copy-start(f32[64,8,4,128]{3,1,2,0:T(8,128)} %copy.80) | copy-start | bytes 3145732
  243.1 9.2 %copy-start.2 = (bf16[1,512,2,128]{3,2,1,0:T(2,128)(2,1)S(1)}, bf16[1,512,2,128]{3,2,1,0:T(2,128)(2,1)}, u32[]{:S(2)}) copy-start(bf16[1,512,2,128]{3,2,1,0:T(2,128)(2,1)} %get-tuple-element.195) | copy-start | bytes 786436
  243.9 12.4 %all-to-all-start.1 = ((bf16[128,4,2,128]{3,0,2,1:T(8,128)(2,1)}), bf16[128,4,2,128]{3,0,2,1:T(8,128)(2,1)S(1)}, u32[]{:S(2)}, u32[]{:S(2)}) async-start(bf16[128,4,2,128]{3,0,2,1:T(8,128)(2,1)} %copy.51), calls=%async_computation.1 | async-start | bytes 524288 | tf_op jit(solution)/shard_map/all_to_all | solution.py:97
  250.5 32.4 %all-gather.9.cloned.1.call-start = ((), (), s32[]{:S(2)}) async-start(), calls=%async_computation.4 | async-start | bytes 2621440 | tf_op jit(solution)/shard_map/all_gather | solution.py:127
  257.7 87.5 %all-gather.7.cloned.1.call-start = ((), (), s32[]{:S(2)}) async-start(), calls=%async_computation.3 | async-start | bytes 3932160 | tf_op jit(solution)/shard_map/all_gather | solution.py:53
Sparse Core Ops, SparseCore 0:
  8.9 164.8 all-gather.4
  257.8 25.0 all-gather.8
  284.5 60.6 all-gather.6
where the time goes:
time: 361 us; the launch traced here: 356 us
  waiting for transfers between devices  268 us (74%)
  local copies, waits for them, and re-layouts  28.3 us (8%)
  matrix products  21.3 us (6%)
  starting transfers between devices  19.4 us (5%)
  between operations  13.3 us (4%)
  other arithmetic  5.57 us (2%)
    all_gather x1, waiting for transfers between devices, shards(): piece = lax.all_gather(w_qkv, 'seq', axis=0, tiled=True)  163 us
    all_gather x1, waiting for transfers between devices, shards(): whole_out = lax.all_gather(w_out, 'seq', axis=0, tiled=True)  59.4 us
    all_gather x1, waiting for transfers between devices, shards(): lax.all_gather(attention, ('head', 'sub'), axis=1, tiled=True)  24.5 us
    all_to_all x1, waiting for transfers between devices, shards(): lax.all_to_all(temporal_in, 'seq', split_axis=0, concat_axis=1, tiled=True)  17.5 us
    unnamed x20, local copies, waits for them, and re-layouts  10.5 us
    dot_general x1, matrix products, shards(): jnp.dot(hidden, piece.reshape(piece.shape[0], -1), preferred_element_type...  10 us
  transfers between devices with their start and end apart: 7, of which 6 were waited for; matrix products, arithmetic and copies ran while one was open for 4% of the time, Pallas kernels for 0%

commit v1 on v0

--- a/solution.py
+++ b/solution.py
@@ -1,8 +1,11 @@
+import functools
 import math
 
 import jax
 import jax.numpy as jnp
 from jax import lax
+from jax.experimental import pallas as pl
+from jax.experimental.pallas import tpu as pltpu
 from jax.sharding import PartitionSpec as P
 
 BLOCK = 128
@@ -29,6 +32,325 @@
     return cells
 
 
+MESH = pl.DeviceIdType.MESH
+
+
+def pieces_of(rows, most=4):
+    for count in range(most, 0, -1):
+        if rows % (16 * count) == 0:
+            return count
+    return 1
+
+
+class LineGather:
+    def __init__(self, own, slots, sems, chunks, count, parts):
+        self.own, self.slots, self.chunks = own, slots, chunks
+        self.sems, self.count, self.parts = sems, count, parts
+        self.me = lax.axis_index("seq")
+        self.group = lax.axis_index("groups")
+        self.size = own.shape[0] // (parts * chunks)
+
+    def rows(self, group, chunk):
+        start = (group * self.chunks + chunk) * self.size
+        return pl.ds(pl.multiple_of(start, self.size), self.size)
+
+    def along(self, shard, chunk, way, own):
+        rows = self.rows(self.group, chunk)
+        source = self.own.at[rows] if own else self.slots.at[shard, rows]
+        return pltpu.make_async_remote_copy(
+            src_ref=source,
+            dst_ref=self.slots.at[shard, rows],
+            send_sem=self.sems.at[way, 0, shard, chunk],
+            recv_sem=self.sems.at[way, 1, shard, chunk],
+            device_id={"seq": self.me + (1 if way == 0 else -1)},
+            device_id_type=MESH,
+        )
+
+    def across(self, shard, chunk, hop):
+        rows = self.rows(self.group, chunk)
+        return pltpu.make_async_remote_copy(
+            src_ref=self.slots.at[shard, rows],
+            dst_ref=self.slots.at[shard, rows],
+            send_sem=self.sems.at[1 + hop, 0, shard, chunk],
+            recv_sem=self.sems.at[1 + hop, 1, shard, chunk],
+            device_id={"groups": lax.rem(self.group + hop, self.parts)},
+            device_id_type=MESH,
+        )
+
+    def open_line(self):
+        for chunk in range(self.chunks):
+            for way in (0, 1):
+                @pl.when(self.onward(way))
+                def _():
+                    self.along(self.me, chunk, way, True).start()
+
+    def onward(self, way):
+        return self.me < self.count - 1 if way == 0 else self.me > 0
+
+    def shard_of(self, step, way):
+        return self.me - step if way == 0 else self.me + step
+
+    def present(self, step, way):
+        return self.me >= step if way == 0 else self.me + step < self.count
+
+    def relay(self, step):
+        for chunk in range(self.chunks):
+            for way in (0, 1):
+                shard = self.shard_of(step, way)
+
+                @pl.when(self.present(step, way))
+                def _():
+                    self.along(shard, chunk, way, False).wait_recv()
+
+                    @pl.when(self.onward(way))
+                    def _():
+                        self.along(shard, chunk, way, False).start()
+
+                    for hop in range(1, self.parts):
+                        self.across(shard, chunk, hop).start()
+
+    def complete(self, shard):
+        for chunk in range(self.chunks):
+            for hop in range(1, self.parts):
+                self.across(shard, chunk, hop).wait_recv()
+
+    def close_sends(self, step):
+        for chunk in range(self.chunks):
+            for way in (0, 1):
+                shard = self.shard_of(step, way)
+
+                @pl.when(self.present(step, way))
+                def _():
+                    @pl.when(self.onward(way))
+                    def _():
+                        self.along(shard, chunk, way, False).wait_send()
+
+                    for hop in range(1, self.parts):
+                        self.across(shard, chunk, hop).wait_send()
+
+    def close_own(self):
+        for chunk in range(self.chunks):
+            for way in (0, 1):
+                @pl.when(self.onward(way))
+                def _():
+                    self.along(self.me, chunk, way, True).wait_send()
+
+
+def project_kernel(count, parts, q_chunks, o_chunks, hidden, w_own, o_own, qkv, o_all, slots, total, q_sems, o_sems, own_sem):
+    me = lax.axis_index("seq")
+    group = lax.axis_index("groups")
+    barrier = pltpu.get_barrier_semaphore()
+
+    @pl.when(me > 0)
+    def _():
+        pl.semaphore_signal(barrier, inc=1, device_id={"seq": me - 1}, device_id_type=MESH)
+
+    @pl.when(me < count - 1)
+    def _():
+        pl.semaphore_signal(barrier, inc=1, device_id={"seq": me + 1}, device_id_type=MESH)
+
+    for hop in range(1, parts):
+        pl.semaphore_signal(
+            barrier, inc=1, device_id={"groups": lax.rem(group + hop, parts)}, device_id_type=MESH
+        )
+    neighbours = jnp.where(me > 0, 1, 0) + jnp.where(me < count - 1, 1, 0) + (parts - 1)
+    pl.semaphore_wait(barrier, neighbours)
+
+    line = LineGather(w_own, slots, q_sems, q_chunks, count, parts)
+    outs = LineGather(o_own, o_all, o_sems, o_chunks, count, parts)
+    line.open_line()
+    keep = pltpu.make_async_copy(o_own, o_all.at[me], own_sem)
+    keep.start()
+    tile = 256
+
+    def add(shard, block, first):
+        def column(j, carry):
+            at = pl.ds(pl.multiple_of(j * tile, tile), tile)
+            product = jnp.dot(hidden[shard], block[:, at], preferred_element_type=jnp.float32)
+            total[:, at] = product if first else total[:, at] + product
+            return carry
+
+        lax.fori_loop(0, total.shape[1] // tile, column, 0)
+
+    def finish(step):
+        for way in (0, 1):
+            shard = line.shard_of(step, way)
+
+            @pl.when(line.present(step, way))
+            def _():
+                line.complete(shard)
+                add(shard, slots.at[shard], False)
+
+    add(me, w_own, True)
+
+    def q_step(step, carry):
+        line.relay(step)
+
+        @pl.when(step > 1)
+        def _():
+            finish(step - 1)
+
+        return carry
+
+    lax.fori_loop(1, count, q_step, 0)
+    outs.open_line()
+    finish(count - 1)
+    qkv[...] = total[...].astype(qkv.dtype)
+
+    def o_step(step, carry):
+        outs.relay(step)
+        return carry
+
+    lax.fori_loop(1, count, o_step, 0)
+
+    def last(step, carry):
+        line.close_sends(step)
+        outs.close_sends(step)
+        for way in (0, 1):
+            shard = outs.shard_of(step, way)
+
+            @pl.when(outs.present(step, way))
+            def _():
+                outs.complete(shard)
+
+        return carry
+
+    lax.fori_loop(1, count, last, 0)
+    line.close_own()
+    outs.close_own()
+    keep.wait()
+
+
+def project(hidden, w_own, o_own):
+    count, parts = lax.axis_size("seq"), lax.axis_size("groups")
+    rows, depth = hidden.shape
+    hidden = hidden.reshape(rows, count, depth // count).transpose(1, 0, 2)
+    width = w_own.shape[1]
+    most = 4 if count <= 8 else 1
+    q_chunks = pieces_of(w_own.shape[0] // parts, most)
+    o_chunks = pieces_of(o_own.shape[0] // parts, most)
+    vmem = pl.BlockSpec(memory_space=pltpu.VMEM)
+    return pl.pallas_call(
+        functools.partial(project_kernel, count, parts, q_chunks, o_chunks),
+        out_shape=[
+            jax.ShapeDtypeStruct((rows, width), jnp.bfloat16),
+            jax.ShapeDtypeStruct((count,) + o_own.shape, jnp.bfloat16),
+        ],
+        in_specs=[vmem] * 3,
+        out_specs=[vmem, pl.BlockSpec(memory_space=pl.ANY)],
+        scratch_shapes=[
+            pltpu.VMEM((count,) + w_own.shape, jnp.bfloat16),
+            pltpu.VMEM((rows, width), jnp.float32),
+            pltpu.SemaphoreType.DMA((1 + parts, 2, count, q_chunks)),
+            pltpu.SemaphoreType.DMA((1 + parts, 2, count, o_chunks)),
+            pltpu.SemaphoreType.DMA,
+        ],
+        compiler_params=pltpu.CompilerParams(
+            collective_id=0, has_side_effects=True, vmem_limit_bytes=48 * 1024 * 1024
+        ),
+        name="project",
+    )(hidden, w_own, o_own)
+
+
+def mix_kernel(heads, subs, chunks, attn, w_all, gate, update, slots, total, x_sems, c_sems):
+    head, sub = lax.axis_index("head"), lax.axis_index("sub")
+    barrier = pltpu.get_barrier_semaphore()
+    for hop in range(1, heads):
+        pl.semaphore_signal(
+            barrier, inc=1, device_id={"head": lax.rem(head + hop, heads)}, device_id_type=MESH
+        )
+    for hop in range(1, subs):
+        pl.semaphore_signal(
+            barrier, inc=1, device_id={"sub": lax.rem(sub + hop, subs)}, device_id_type=MESH
+        )
+    pl.semaphore_wait(barrier, heads + subs - 2)
+    size = attn.shape[0] // chunks
+
+    def to_head(hop, chunk):
+        rows = pl.ds(chunk * size, size)
+        return pltpu.make_async_remote_copy(
+            src_ref=attn.at[rows],
+            dst_ref=slots.at[hop, 0, rows],
+            send_sem=x_sems.at[hop, 0, chunk],
+            recv_sem=x_sems.at[hop, 1, chunk],
+            device_id={"head": lax.rem(head + hop, heads)},
+            device_id_type=MESH,
+        )
+
+    def to_sub(hop, turn, chunk):
+        rows = pl.ds(chunk * size, size)
+        return pltpu.make_async_remote_copy(
+            src_ref=attn.at[rows] if hop == 0 else slots.at[hop, 0, rows],
+            dst_ref=slots.at[hop, turn, rows],
+            send_sem=c_sems.at[hop, turn, 0, chunk],
+            recv_sem=c_sems.at[hop, turn, 1, chunk],
+            device_id={"sub": lax.rem(sub + turn, subs)},
+            device_id_type=MESH,
+        )
+
+    for chunk in range(chunks):
+        for hop in range(1, heads):
+            to_head(hop, chunk).start()
+        for turn in range(1, subs):
+            to_sub(0, turn, chunk).start()
+
+    def add(chunk, hop, turn, first):
+        rows = slice(chunk * size, (chunk + 1) * size)
+        owner = lax.rem(head + heads - hop, heads) * subs + lax.rem(sub + subs - turn, subs)
+        block = attn[rows, :] if hop == 0 and turn == 0 else slots[hop, turn, rows, :]
+        product = jnp.dot(block, w_all[owner], preferred_element_type=jnp.float32)
+        total[rows, :] = product if first else total[rows, :] + product
+
+    for chunk in range(chunks):
+        add(chunk, 0, 0, True)
+    for chunk in range(chunks):
+        for turn in range(1, subs):
+            to_sub(0, turn, chunk).wait_recv()
+            add(chunk, 0, turn, False)
+    for chunk in range(chunks):
+        for hop in range(1, heads):
+            to_head(hop, chunk).wait_recv()
+            for turn in range(1, subs):
+                to_sub(hop, turn, chunk).start()
+            add(chunk, hop, 0, False)
+    for chunk in range(chunks):
+        for hop in range(1, heads):
+            for turn in range(1, subs):
+                to_sub(hop, turn, chunk).wait_recv()
+                add(chunk, hop, turn, False)
+        rows = slice(chunk * size, (chunk + 1) * size)
+        update[rows, :] = (gate[...] * total[rows, :]).astype(update.dtype)
+    for chunk in range(chunks):
+        for hop in range(1, heads):
+            to_head(hop, chunk).wait_send()
+        for hop in range(heads):
+            for turn in range(1, subs):
+                to_sub(hop, turn, chunk).wait_send()
+
+
+def mix(attention, w_all, gate):
+    heads, subs = lax.axis_size("head"), lax.axis_size("sub")
+    rows, width = attention.shape
+    chunks = pieces_of(rows, 2)
+    vmem = pl.BlockSpec(memory_space=pltpu.VMEM)
+    return pl.pallas_call(
+        functools.partial(mix_kernel, heads, subs, chunks),
+        out_shape=jax.ShapeDtypeStruct((rows, w_all.shape[-1]), jnp.bfloat16),
+        in_specs=[vmem] * 3,
+        out_specs=vmem,
+        scratch_shapes=[
+            pltpu.VMEM((heads, subs, rows, width), jnp.bfloat16),
+            pltpu.VMEM((rows, w_all.shape[-1]), jnp.float32),
+            pltpu.SemaphoreType.DMA((heads, 2, chunks)),
+            pltpu.SemaphoreType.DMA((heads, subs, 2, chunks)),
+        ],
+        compiler_params=pltpu.CompilerParams(
+            collective_id=1, has_side_effects=True, vmem_limit_bytes=40 * 1024 * 1024
+        ),
+        name="mix",
+    )(attention, w_all, gate)
+
+
 def modulate(tokens, modulation):
     values = tokens.astype(jnp.float32)
     center = jnp.mean(values, axis=-1, keepdims=True)
@@ -46,12 +368,8 @@
     slot_total = pattern.shape[1]
     scale_factor = 1.0 / math.sqrt(head_size)
     hidden = modulate(tokens, modulation)
-    piece = lax.all_gather(w_qkv, "seq", axis=0, tiled=True)
-    projected = jnp.dot(
-        hidden, piece.reshape(piece.shape[0], -1), preferred_element_type=jnp.float32
-    )
-    whole_out = lax.all_gather(w_out, "seq", axis=0, tiled=True)
-    packed = projected.astype(jnp.bfloat16).reshape(
+    projected, whole_out = project(hidden, w_qkv.reshape(w_qkv.shape[0], -1), w_out)
+    packed = projected.reshape(
         frames_local, positions, pairs_local, 6 * head_size
     )
     temporal_in = packed[..., : 3 * head_size].transpose(1, 0, 2, 3)
@@ -121,17 +439,13 @@
     )
     spatial_out = (numerator / denominator.transpose(0, 2, 1)[..., None]).astype(jnp.bfloat16)
     attention = jnp.concatenate([temporal_out.transpose(1, 0, 2, 3), spatial_out], axis=-1)
-    attention = attention.reshape(row_count, pairs_local, 2 * head_size)
-    out_width = whole_out.shape[1]
-    mixed = jnp.dot(
-        lax.all_gather(attention, ("head", "sub"), axis=1, tiled=True).reshape(row_count, -1),
-        whole_out,
-        preferred_element_type=jnp.float32,
-    )
+    attention = attention.reshape(row_count, pairs_local * 2 * head_size)
+    out_width = w_out.shape[1]
+    blocks = lax.axis_size("head") * lax.axis_size("sub")
     gate_slice = lax.dynamic_slice_in_dim(
         modulation[2], lax.axis_index(("head", "sub")) * out_width, out_width, 0
     )
-    return (gate_slice * mixed).astype(jnp.bfloat16)
+    return mix(attention, whole_out.reshape(blocks, -1, out_width), gate_slice[None, :])
 
 
 def solution(mesh):

time: 361 us -> 214 us (0.59)
  waiting for transfers between devices: 268 us -> 15.8 us
  Pallas kernels: 0 us -> 137 us
  matrix products: 21.3 us -> 7.66 us
  between operations: 13.3 us -> 0.25 us
    all_gather x3 -> x0, waiting for transfers between devices: 247 us -> none  [the longest x1 163 us: shards(): piece = lax.all_gather(w_qkv, 'seq', axis=0, tiled=True)]
    pallas_call x0 -> x2, Pallas kernels: none -> 137 us  [the longest x1 116 us: project(): pl.pallas_call(functools.partial(project_kernel, count, parts, q_chunks,...]
    dot_general x2 -> x0, matrix products: 14.6 us -> none  [the longest x1 10 us: shards(): jnp.dot(hidden, piece.reshape(piece.shape[0], -1), preferred_element_type...]
    unnamed x20 -> x32, local copies, waits for them, and re-layouts: 10.5 us -> 6.71 us
    reshape x1 -> x3, local copies, waits for them, and re-layouts: 3.63 us -> 7.27 us  [the longest x1 4.81 us: project(): hidden = hidden.reshape(rows, count, depth // count).transpose(1, 0, 2)]
  transfers between devices with their start and end apart: 7 -> 4, of which waited for: 6 -> 3; matrix products, arithmetic and copies ran while one was open for 4% -> 3% of each run, Pallas kernels for 0% -> 0%
where the time goes in v1:
time: 214 us; the launch traced here: 211 us
  Pallas kernels  137 us (64%)
  local copies, waits for them, and re-layouts  25.9 us (12%)
  starting transfers between devices  16 us (7%)
  waiting for transfers between devices  15.8 us (7%)
  other arithmetic  7.94 us (4%)
  matrix products  7.66 us (4%)
    pallas_call x1, Pallas kernels, project(): pl.pallas_call(functools.partial(project_kernel, count, parts, q_chunks,...  116 us
    pallas_call x1, Pallas kernels, mix(): pl.pallas_call(functools.partial(mix_kernel, heads, subs, chunks), out_sh...  21.5 us
    all_to_all x1, waiting for transfers between devices, shards(): lax.all_to_all(temporal_in, 'seq', split_axis=0, concat_axis=1, tiled=True)  14.4 us
    unnamed x32, local copies, waits for them, and re-layouts  6.71 us
    all_to_all x1, starting transfers between devices, shards(): lax.all_to_all(outcome, 'seq', split_axis=1, concat_axis=0, tiled=True)  5.48 us
    reshape x1, local copies, waits for them, and re-layouts, project(): hidden = hidden.reshape(rows, count, depth // count).transpose(1, 0, 2)  4.81 us
    ppermute x1, starting transfers between devices, with_halo(): lax.ppermute(head, axis, [((i + 1) % count, i) for i in range(ends)])  4.7 us
    all_to_all x1, starting transfers between devices, shards(): lax.all_to_all(temporal_in, 'seq', split_axis=0, concat_axis=1, tiled=True)  4.54 us
  transfers between devices with their start and end apart: 4, of which 3 were waited for; matrix products, arithmetic and copies ran while one was open for 3% of the time, Pallas kernels for 0%

profile of v1, /device:TPU:25, one launch (start us, length us, event | category | flops | bytes accessed | tf_op | source)
XLA Modules:
  0.0 211.2 jit_solution(10886123034780823020)
XLA Ops:
  0.0 3.2 %copy.35 = bf16[512,3072]{0,1:T(8,128)(2,1)S(1)} copy(bf16[512,3072]{1,0:T(8,128)(2,1)} %param.9) | data formatting | bytes 6291456 | tf_op args[0]
  3.2 0.5 convert_reduce_fusion
  3.7 0.9 fusion.8
  4.6 2.8 %fusion.11 = bf16[512,3072]{0,1:T(8,128)(2,1)} fusion(bf16[512,3072]{0,1:T(8,128)(2,1)S(1)} %copy.35, f32[3072]{0:T(1024)S(1)} %bitcast.91, f32[3072]{0:T(1024)S(1)} %bitcast.90, f32[512]{0:T(512)S(1)} %add_rsqrt_fusion, f32[512]{0:T(512)S(1)} %broadcast_multiply_fusion), kind=kLoop, calls=%fused_computation.22 | loop fusion | flops 9437184 | bytes 6320128 | tf_op jit(solution)/shard_map/convert_element_type | solution.py:359
  7.5 4.8 %copy.36 = bf16[512,4,768]{2,0,1:T(8,128)(2,1)} copy(bf16[512,4,768]{0,2,1:T(8,128)(2,1)} %bitcast.77) | data formatting | bytes 6291456 | tf_op jit(solution)/shard_map/reshape | solution.py:227
  12.3 0.4 copy.56
  12.7 0.7 copy-done.2
  13.4 115.8 %project.1 = (bf16[512,1536]{1,0:T(8,128)(2,1)S(1)}, bf16[4,512,768]{2,1,0:T(8,128)(2,1)}) custom-call(bf16[4,512,768]{2,1,0:T(8,128)(2,1)} %bitcast.76, bf16[768,1536]{1,0:T(8,128)(2,1)S(1)} %bitcast.75, bf16[512,768]{1,0:T(8,128)(2,1)S(1)} %copy-done.2), custom_call_target="tpu_custom_call" | custom-call | tf_op jit(solution)/shard_map/project/pallas_call | solution.py:233
  129.2 0.4 reshape.86
  129.6 1.4 slice_bitcast_fusion
  131.0 4.5 %all-to-all-start = ((bf16[512,1,2,384]{3,2,1,0:T(2,128)(2,1)}), bf16[512,1,2,384]{3,2,1,0:T(2,128)(2,1)S(1)}, u32[]{:S(2)}, u32[]{:S(2)}) async-start(bf16[512,1,2,384]{3,2,1,0:T(2,128)(2,1)} %slice_bitcast_fusion), calls=%async_computation | async-start | bytes 1572864 | tf_op jit(solution)/shard_map/all_to_all | solution.py:376
  135.7 0.2 mul.97
  136.0 1.3 fusion.24
  137.3 14.4 %all-to-all-done = bf16[512,1,2,384]{3,2,1,0:T(2,128)(2,1)S(1)} async-done(((bf16[512,1,2,384]{3,2,1,0:T(2,128)(2,1)}), bf16[512,1,2,384]{3,2,1,0:T(2,128)(2,1)S(1)}, u32[]{:S(2)}, u32[]{:S(2)}) %all-to-all-start) | async-done | bytes 786464 | tf_op jit(solution)/shard_map/all_to_all | solution.py:376
  151.7 1.5 copy.72
  153.2 1.6 reshape.87
  154.8 0.7 fusion.25
  155.5 1.3 collective-permute-start
  156.8 4.7 %collective-permute-start.1 = (bf16[256,2,256]{2,0,1:T(8,128)(2,1)S(1)}, bf16[256,2,256]{2,0,1:T(8,128)(2,1)}, u32[]{:S(2)}, u32[]{:S(2)}) collective-permute-start(bf16[256,2,256]{2,0,1:T(8,128)(2,1)S(1)} %get-tuple-element.196), channel_id=1, source_target_pairs={{4,0},{8,4},{12,8},{5,1},{9,5},{13,9},{6,2},{10,6},{14,10},{7,3},{... | collective-permute-start | bytes 786440 | tf_op jit(solution)/shard_map/ppermute | solution.py:28
  161.5 1.9 fusion.12
  163.5 0.2 copy.53
  163.8 0.3 collective-permute-done.1
  164.1 1.1 pad_maximum_fusion
  165.3 5.9 %while.16 = (s32[]{:T(128)}, f32[4,2,128,128]{3,2,1,0:T(8,128)S(1)}, f32[4,2,128]{2,1,0:T(2,128)S(1)}, s32[4,4]{0,1:T(4,128)S(1)}, bf16[8,128,2,256]{3,1,2,0:T(8...) while((s32[]{:T(128)}, ...), condition=%wide.region_4.5_spmd.clone, body=%wide.region_2.4_spmd.clone.sunk | while | flops 68159520 | bytes 4477656 | solution.py:412
  165.3 0.6 gather_fusion
  166.1 0.3 fusion.36
  166.4 0.3 convolution_add_fusion.2
  166.8 0.6 gather_fusion
  167.5 0.3 fusion.36
  167.9 0.3 convolution_add_fusion.2
  168.3 0.6 gather_fusion
  169.0 0.3 fusion.36
  169.4 0.3 convolution_add_fusion.2
  169.8 0.6 gather_fusion
  170.5 0.3 fusion.36
  170.8 0.3 convolution_add_fusion.2
  171.2 0.2 fusion.19
  171.4 0.7 copy.42
  172.2 5.5 %all-to-all-start.1 = ((bf16[128,4,2,128]{3,0,2,1:T(8,128)(2,1)}), bf16[128,4,2,128]{3,0,2,1:T(8,128)(2,1)S(1)}, u32[]{:S(2)}, u32[]{:S(2)}) async-start(bf16[128,4,2,128]{3,0,2,1:T(8,128)(2,1)} %copy.42), calls=%async_computation.1 | async-start | bytes 524288 | tf_op jit(solution)/shard_map/all_to_all | solution.py:415
  177.7 3.1 %fusion.15 = bf16[1,512,2,128]{1,3,2,0:T(8,128)(2,1)} fusion(f32[2,512,512]{1,2,0:T(8,128)} %get-tuple-element.201, f32[512,512]{0,1:T(8,128)} %bitcast.81, bf16[1,512,2,128]{1,3,2,0:T(8,128)(2,1)S(1)} %copy.53, f32[512,2]{0,1:T(2,128)S(1)} %bitcast.92), kind=kOutput, calls=%fused_computation.28 | convolution fusion | flops 136052736 | bytes 3674112 | tf_op jit(solution)/shard_map/fnpq,fqnc->fpnc/dot_general | solution.py:434
  180.7 1.2 all-to-all-done.1
  181.9 0.9 copy.43
  182.8 1.1 transpose.43
  183.8 1.8 pad_maximum_fusion.1
  185.6 2.1 copy.52.attn
  187.7 1.0 copy-done.1
  188.7 21.5 %mix.1 = bf16[512,768]{1,0:T(8,128)(2,1)S(1)} custom-call(bf16[512,512]{1,0:T(8,128)(2,1)S(1)} %copy-done.1, bf16[4,512,768]{2,1,0:T(8,128)(2,1)S(1)} %copy-done, f32[1,768]{1,0:T(1,128)S(1)} %constant_dynamic-slice_fusion.gate), custom_call_target="tpu_custom_call" | custom-call | tf_op jit(solution)/shard_map/mix/pallas_call | solution.py:336
  210.3 0.9 copy.83
  (59 shorter events, 1.1 us)
Async XLA Ops:
  3.7 0.9 copy-start.8
  7.5 4.8 %copy-start.4 = (bf16[768,2,768]{2,1,0:T(2,128)(2,1)S(1)}, bf16[768,2,768]{2,1,0:T(2,128)(2,1)}, u32[]{:S(2)}) copy-start(bf16[768,2,768]{2,1,0:T(2,128)(2,1)} %param.11) | copy-start | bytes 7077892
  12.3 1.1 copy-start.2
  129.6 6.0 %copy-start.9 = (s32[1,4,4]{2,1,0:T(4,128)S(1)}, s32[1,4,4]{2,1,0:T(4,128)}, u32[]{:S(2)}) copy-start(s32[1,4,4]{2,1,0:T(4,128)} %param.15) | copy-start | bytes 196
  131.0 20.7 %all-to-all-start = ((bf16[512,1,2,384]{3,2,1,0:T(2,128)(2,1)}), bf16[512,1,2,384]{3,2,1,0:T(2,128)(2,1)S(1)}, u32[]{:S(2)}, u32[]{:S(2)}) async-start(bf16[512,1,2,384]{3,2,1,0:T(2,128)(2,1)} %slice_bitcast_fusion), calls=%async_computation | async-start | bytes 1572864 | tf_op jit(solution)/shard_map/all_to_all | solution.py:376
  136.0 25.5 %copy-start.3 = (f32[64,8,4,128]{3,1,2,0:T(8,128)}, f32[64,8,4,128]{3,1,2,0:T(8,128)S(1)}, u32[]{:S(2)}) copy-start(f32[64,8,4,128]{3,1,2,0:T(8,128)S(1)} %copy.71) | copy-start | bytes 3145732
  137.3 24.2 %copy-start.5 = (bf16[1,512,2,128]{3,2,1,0:T(2,128)(2,1)S(1)}, bf16[1,512,2,128]{3,2,1,0:T(2,128)(2,1)}, u32[]{:S(2)}) copy-start(bf16[1,512,2,128]{3,2,1,0:T(2,128)(2,1)} %get-tuple-element.193) | copy-start | bytes 786436
  137.3 24.2 %copy-start.6 = (bf16[1,512,2,128]{3,2,1,0:T(2,128)(2,1)S(1)}, bf16[1,512,2,128]{3,2,1,0:T(2,128)(2,1)}, u32[]{:S(2)}) copy-start(bf16[1,512,2,128]{3,2,1,0:T(2,128)(2,1)} %get-tuple-element.194) | copy-start | bytes 786436
  154.7 8.6 %copy-start.10 = (s32[4,4]{1,0:T(4,128)S(1)}, s32[4,4]{1,0:T(4,128)}, u32[]{:S(2)}) copy-start(s32[4,4]{1,0:T(4,128)} %param.13) | copy-start | bytes 196
  154.8 8.7 %copy-start.7 = (bf16[1,512,2,128]{3,2,1,0:T(2,128)(2,1)S(1)}, bf16[1,512,2,128]{3,2,1,0:T(2,128)(2,1)}, u32[]{:S(2)}) copy-start(bf16[1,512,2,128]{3,2,1,0:T(2,128)(2,1)} %get-tuple-element.192) | copy-start | bytes 786436
  155.5 8.3 %collective-permute-start = (bf16[256,2,256]{2,0,1:T(8,128)(2,1)}, bf16[256,2,256]{2,0,1:T(8,128)(2,1)}, u32[]{:S(2)}, u32[]{:S(2)}) collective-permute-start(bf16[256,2,256]{2,0,1:T(8,128)(2,1)} %get-tuple-element.195), channel_id=1, source_target_pairs={{0,4},{4,8},{8,12},{1,5},{5,9},{9,13},{2,6},{6,10},{10,14},{3,7},{... | collective-permute-start | bytes 786440 | tf_op jit(solution)/shard_map/ppermute | solution.py:26
  156.8 7.3 %collective-permute-start.1 = (bf16[256,2,256]{2,0,1:T(8,128)(2,1)S(1)}, bf16[256,2,256]{2,0,1:T(8,128)(2,1)}, u32[]{:S(2)}, u32[]{:S(2)}) collective-permute-start(bf16[256,2,256]{2,0,1:T(8,128)(2,1)S(1)} %get-tuple-element.196), channel_id=1, source_target_pairs={{4,0},{8,4},{12,8},{5,1},{9,5},{13,9},{6,2},{10,6},{14,10},{7,3},{... | collective-permute-start | bytes 786440 | tf_op jit(solution)/shard_map/ppermute | solution.py:28
  163.8 1.5 copy-start.11
  172.2 9.7 %all-to-all-start.1 = ((bf16[128,4,2,128]{3,0,2,1:T(8,128)(2,1)}), bf16[128,4,2,128]{3,0,2,1:T(8,128)(2,1)S(1)}, u32[]{:S(2)}, u32[]{:S(2)}) async-start(bf16[128,4,2,128]{3,0,2,1:T(8,128)(2,1)} %copy.42), calls=%async_computation.1 | async-start | bytes 524288 | tf_op jit(solution)/shard_map/all_to_all | solution.py:415
  180.7 6.9 %copy-start = (bf16[4,512,768]{2,1,0:T(8,128)(2,1)S(1)}, bf16[4,512,768]{2,1,0:T(8,128)(2,1)}, u32[]{:S(2)}) copy-start(bf16[4,512,768]{2,1,0:T(8,128)(2,1)} %get-tuple-element.135.w_all) | copy-start | bytes 9437188
  187.7 1.0 copy-start.1

commit v2 on v1

--- a/solution.py
+++ b/solution.py
@@ -447,10 +447,494 @@
     )
     return mix(attention, whole_out.reshape(blocks, -1, out_width), gate_slice[None, :])
 
+def meet(axes):
+    barrier = pltpu.get_barrier_semaphore()
+    others = 0
+    for axis in axes:
+        size = lax.axis_size(axis)
+        for hop in range(1, size):
+            other = lax.rem(lax.axis_index(axis) + hop, size)
+            pl.semaphore_signal(barrier, inc=1, device_id={axis: other}, device_id_type=MESH)
+            others += 1
+    pl.semaphore_wait(barrier, others)
+
+
+def push(source, target, send_sem, recv_sem, axis, place):
+    return pltpu.make_async_remote_copy(
+        src_ref=source,
+        dst_ref=target,
+        send_sem=send_sem,
+        recv_sem=recv_sem,
+        device_id={axis: place},
+        device_id_type=MESH,
+    )
+
+
+def by_head_kernel(
+    sizes, chunks, o_chunks, span, hid_own, w_parts, o_own, lists, blocks, o_all, lists_all,
+    hfull, wfull, w_sems, l_sems, z_sems, x_sems, c_sems, o_sems, own_sems,
+):
+    count, parts, heads, subs = sizes
+    me, group = lax.axis_index("seq"), lax.axis_index("groups")
+    head, sub = lax.axis_index("head"), lax.axis_index("sub")
+    meet(("seq", "groups", "head", "sub"))
+    quarter = hid_own.shape[0]
+    size = quarter // chunks
+    half = w_parts.shape[1] // parts
+    mine = pl.ds(pl.multiple_of(group * half, half), half)
+
+    def place(hop, axis, size_):
+        return lax.rem(lax.axis_index(axis) + hop, size_)
+
+    def source_of(hop):
+        return lax.rem(me + count - hop, count)
+
+    def w_along(hop, shard):
+        return push(
+            w_parts.at[place(hop, "seq", count), mine], wfull.at[shard, mine],
+            w_sems.at[0, 0, hop], w_sems.at[0, 1, hop], "seq", place(hop, "seq", count),
+        )
+
+    def w_across(hop, turn):
+        spot = wfull.at[source_of(hop), mine]
+        return push(
+            spot, spot, w_sems.at[turn, 0, hop], w_sems.at[turn, 1, hop],
+            "groups", place(turn, "groups", parts),
+        )
+
+    def l_along(hop):
+        return push(
+            lists, lists_all.at[me], l_sems.at[0, hop], l_sems.at[1, hop],
+            "seq", place(hop, "seq", count),
+        )
+
+    def rows_of(head_hop, sub_hop, chunk):
+        owner = lax.rem(head + heads - head_hop, heads) * subs + lax.rem(sub + subs - sub_hop, subs)
+        return pl.ds(pl.multiple_of(owner * quarter + chunk * size, size), size)
+
+    def spot(shard, head_hop, sub_hop, chunk):
+        return hfull.at[shard, rows_of(head_hop, sub_hop, chunk)]
+
+    def z_push(shard, chunk, way, own):
+        target = spot(shard, 0, 0, chunk)
+        return push(
+            hid_own.at[pl.ds(chunk * size, size)] if own else target, target,
+            z_sems.at[way, 0, shard, chunk], z_sems.at[way, 1, shard, chunk],
+            "seq", me + (1 if way == 0 else -1),
+        )
+
+    def x_push(shard, chunk, hop, own=False):
+        target = spot(shard, 0, 0, chunk)
+        return push(
+            hid_own.at[pl.ds(chunk * size, size)] if own else target, target,
+            x_sems.at[hop, 0, shard, chunk], x_sems.at[hop, 1, shard, chunk],
+            "head", place(hop, "head", heads),
+        )
+
+    def c_push(shard, chunk, hop, turn, own=False):
+        target = spot(shard, hop, 0, chunk)
+        return push(
+            hid_own.at[pl.ds(chunk * size, size)] if own else target, target,
+            c_sems.at[hop, turn, 0, shard, chunk], c_sems.at[hop, turn, 1, shard, chunk],
+            "sub", place(turn, "sub", subs),
+        )
+
+    outs = LineGather(o_own, o_all, o_sems, o_chunks, count, parts)
+    onward, shard_of, present = outs.onward, outs.shard_of, outs.present
+    ways = lambda step: (0, 1) if step else (0,)
+
+    for hop in range(1, count):
+        l_along(hop).start()
+    for hop in range(1, count):
+        w_along(hop, me).start()
+    for chunk in range(chunks):
+        for way in (0, 1):
+            @pl.when(onward(way))
+            def _():
+                z_push(me, chunk, way, True).start()
+        for hop in range(1, heads):
+            x_push(me, chunk, hop, True).start()
+        for turn in range(1, subs):
+            c_push(me, chunk, 0, turn, True).start()
+    keeps = [
+        pltpu.make_async_copy(o_own, o_all.at[me], own_sems.at[0]),
+        pltpu.make_async_copy(w_parts.at[me], wfull.at[me], own_sems.at[1]),
+        pltpu.make_async_copy(
+            hid_own,
+            hfull.at[me, pl.ds(pl.multiple_of((head * subs + sub) * quarter, quarter), quarter)],
+            own_sems.at[2],
+        ),
+        pltpu.make_async_copy(lists, lists_all.at[me], own_sems.at[3]),
+    ]
+    for keep in keeps:
+        keep.start()
+
+    for hop in range(1, count):
+        w_along(hop, source_of(hop)).wait_recv()
+        for turn in range(1, parts):
+            w_across(hop, turn).start()
+
+    def z_relay(step):
+        for chunk in range(chunks):
+            for way in ways(step):
+                shard = shard_of(step, way)
+
+                @pl.when(present(step, way))
+                def _():
+                    z_push(shard, chunk, way, False).wait_recv()
+
+                    @pl.when(onward(way))
+                    def _():
+                        z_push(shard, chunk, way, False).start()
+
+                    for hop in range(1, heads):
+                        x_push(shard, chunk, hop).start()
+                    for turn in range(1, subs):
+                        c_push(shard, chunk, 0, turn).start()
+
+    def x_relay(step):
+        for chunk in range(chunks):
+            for way in ways(step):
+                shard = shard_of(step, way)
+
+                @pl.when(present(step, way))
+                def _():
+                    for hop in range(1, heads):
+                        x_push(shard, chunk, hop).wait_recv()
+                        for turn in range(1, subs):
+                            c_push(shard, chunk, hop, turn).start()
+
+    def finish(step):
+        for way in ways(step):
+            shard = shard_of(step, way)
+
+            @pl.when(present(step, way))
+            def _():
+                for chunk in range(chunks):
+                    for hop in range(heads):
+                        for turn in range(1, subs):
+                            c_push(shard, chunk, hop, turn).wait_recv()
+                weight = wfull[...].reshape(-1, wfull.shape[-1])
+                total = jnp.dot(hfull[shard], weight, preferred_element_type=jnp.float32)
+                total = total.astype(blocks.dtype)
+                rows = total.shape[0]
+
+                @pl.when(lax.rem(me, 2) == 0)
+                def _():
+                    at = pl.ds(pl.multiple_of(shard * span, span), span)
+                    for i in range(rows // span):
+                        blocks[i, at, :] = total[i * span : (i + 1) * span]
+
+                @pl.when(lax.rem(me, 2) == 1)
+                def _():
+                    each = blocks.shape[1]
+                    for i in range(rows // each):
+                        blocks[shard * (rows // each) + i] = total[i * each : (i + 1) * each]
+
+    for step in range(1, count):
+        z_relay(step)
+        if step == count - 1:
+            outs.open_line()
+        if step == 2:
+            for keep in keeps:
+                keep.wait()
+            for hop in range(1, count):
+                for turn in range(1, parts):
+                    w_across(hop, turn).wait_recv()
+        if step >= 2:
+            x_relay(step - 2)
+            finish(step - 2)
+    x_relay(count - 2)
+    outs.relay(1)
+    finish(count - 2)
+    x_relay(count - 1)
+    finish(count - 1)
+    for step in range(2, count):
+        outs.relay(step)
+
+    for hop in range(1, count):
+        l_along(hop).wait_recv()
+        l_along(hop).wait_send()
+        w_along(hop, me).wait_send()
+        for turn in range(1, parts):
+            w_across(hop, turn).wait_send()
+    for step in range(count):
+        for way in ways(step):
+            shard = shard_of(step, way)
+
+            @pl.when(present(step, way))
+            def _():
+                for chunk in range(chunks):
+                    for side in (0, 1) if step == 0 else (way,):
+                        @pl.when(onward(side))
+                        def _():
+                            z_push(shard, chunk, side, False).wait_send()
+                    for hop in range(1, heads):
+                        x_push(shard, chunk, hop).wait_send()
+                    for hop in range(heads):
+                        for turn in range(1, subs):
+                            c_push(shard, chunk, hop, turn).wait_send()
+    for step in range(1, count):
+        outs.close_sends(step)
+        for way in (0, 1):
+            @pl.when(outs.present(step, way))
+            def _():
+                outs.complete(outs.shard_of(step, way))
+    outs.close_own()
+
+
+def by_head(hid_own, w_parts, o_own, lists, span, block):
+    sizes = tuple(lax.axis_size(axis) for axis in ("seq", "groups", "head", "sub"))
+    count, parts, heads, subs = sizes
+    rows = hid_own.shape[0] * heads * subs
+    depth, width = hid_own.shape[1], w_parts.shape[2]
+    chunks = pieces_of(hid_own.shape[0], 2)
+    o_chunks = pieces_of(o_own.shape[0] // parts, 2)
+    vmem = pl.BlockSpec(memory_space=pltpu.VMEM)
+    dma = pltpu.SemaphoreType.DMA
+    return pl.pallas_call(
+        functools.partial(by_head_kernel, sizes, chunks, o_chunks, span),
+        out_shape=[
+            jax.ShapeDtypeStruct((count * rows // block, block, width), jnp.bfloat16),
+            jax.ShapeDtypeStruct((count,) + o_own.shape, jnp.bfloat16),
+            jax.ShapeDtypeStruct((count,) + lists.shape, lists.dtype),
+        ],
+        in_specs=[vmem] * 4,
+        out_specs=[vmem, pl.BlockSpec(memory_space=pl.ANY), vmem],
+        scratch_shapes=[
+            pltpu.VMEM((count, rows, depth), jnp.bfloat16),
+            pltpu.VMEM((count,) + w_parts.shape[1:], jnp.bfloat16),
+            dma((parts, 2, count)),
+            dma((2, count)),
+            dma((2, 2, count, chunks)),
+            dma((heads, 2, count, chunks)),
+            dma((heads, subs, 2, count, chunks)),
+            dma((1 + parts, 2, count, o_chunks)),
+            dma((4,)),
+        ],
+        compiler_params=pltpu.CompilerParams(
+            collective_id=2, has_side_effects=True, vmem_limit_bytes=48 * 1024 * 1024
+        ),
+        name="by_head",
+    )(hid_own, w_parts, o_own, lists)
+
+
+def attend_kernel(count, span, scale, role, index, alive, blocks, out):
+    total, block, width = blocks.shape
+    size = width // 3
+    slots = index.shape[1]
+    each = total // count
+
+    def query(b, carry):
+        q = blocks[b, :, :size]
+        numerator = jnp.zeros((block, size), jnp.float32)
+        denominator = jnp.zeros((block, 1), jnp.float32)
+        for j in range(slots):
+            at = index[b, j]
+            scores = lax.dot_general(
+                q, blocks[at, :, size : 2 * size], (((1,), (1,)), ((), ())),
+                preferred_element_type=jnp.float32,
+            )
+            weights = jnp.exp(scores * scale) * alive[b, j]
+            denominator = denominator + jnp.sum(weights, axis=-1, keepdims=True)
+            numerator = numerator + jnp.dot(
+                weights.astype(jnp.bfloat16), blocks[at, :, 2 * size :],
+                preferred_element_type=jnp.float32,
+            )
+        result = (numerator / denominator).astype(out.dtype)
+
+        @pl.when(role[0] == 0)
+        def _():
+            at = pl.ds(pl.multiple_of(b * span, span), span)
+            for f in range(count):
+                out[f, at, :] = result[f * span : (f + 1) * span]
+
+        @pl.when(role[0] == 1)
+        def _():
+            at = pl.ds(pl.multiple_of(lax.rem(b, each) * block, block), block)
+            out[b // each, at, :] = result
+
+        return carry
+
+    lax.fori_loop(0, total, query, 0, unroll=2)
+
+
+def attend(role, index, alive, blocks, count, span):
+    total, block, width = blocks.shape
+    size = width // 3
+    smem = pl.BlockSpec(memory_space=pltpu.SMEM)
+    vmem = pl.BlockSpec(memory_space=pltpu.VMEM)
+    return pl.pallas_call(
+        functools.partial(attend_kernel, count, span, 1.0 / math.sqrt(size)),
+        out_shape=jax.ShapeDtypeStruct((count, total * block // count, size), jnp.bfloat16),
+        in_specs=[smem, smem, smem, vmem],
+        out_specs=vmem,
+        name="attend",
+    )(role, index, alive, blocks)
+
+
+def spread_kernel(
+    count, heads, subs, own, w_all, gate, update, slots, total, z_sems, x_sems, c_sems, own_sem
+):
+    me, head, sub = (lax.axis_index(axis) for axis in ("seq", "head", "sub"))
+    meet(("seq", "head", "sub"))
+    size = own.shape[2]
+
+    def columns(step):
+        source = lax.rem(me + count - step, count)
+        return pl.ds(pl.multiple_of(source * size, size), size)
+
+    def spot(hop, turn, step):
+        return slots.at[hop, turn, :, columns(step)]
+
+    def to_seq(step):
+        other = lax.rem(me + step, count)
+        return push(
+            own.at[other], spot(0, 0, 0), z_sems.at[0, step], z_sems.at[1, step], "seq", other
+        )
+
+    def to_head(hop, step):
+        return push(
+            own.at[me] if step == 0 else spot(0, 0, step), spot(hop, 0, step),
+            x_sems.at[hop, 0, step], x_sems.at[hop, 1, step],
+            "head", lax.rem(head + hop, heads),
+        )
+
+    def to_sub(hop, turn, step):
+        return push(
+            own.at[me] if hop == 0 and step == 0 else spot(hop, 0, step), spot(hop, turn, step),
+            c_sems.at[hop, turn, 0, step], c_sems.at[hop, turn, 1, step],
+            "sub", lax.rem(sub + turn, subs),
+        )
+
+    def hand_over(step):
+        for hop in range(1, heads):
+            to_head(hop, step).start()
+        for turn in range(1, subs):
+            to_sub(0, turn, step).start()
+
+    def pass_on(step):
+        for hop in range(1, heads):
+            to_head(hop, step).wait_recv()
+            for turn in range(1, subs):
+                to_sub(hop, turn, step).start()
+
+    for step in range(1, count):
+        to_seq(step).start()
+    hand_over(0)
+    keep = pltpu.make_async_copy(own.at[me], spot(0, 0, 0), own_sem)
+    keep.start()
+    for step in range(1, count):
+        to_seq(step).wait_recv()
+        hand_over(step)
+        pass_on(step - 1)
+    keep.wait()
+
+    def add(hop, turn, first):
+        owner = lax.rem(head + heads - hop, heads) * subs + lax.rem(sub + subs - turn, subs)
+        product = jnp.dot(slots[hop, turn], w_all[owner], preferred_element_type=jnp.float32)
+        total[...] = product if first else total[...] + product
+
+    add(0, 0, True)
+    pass_on(count - 1)
+    for hop in range(heads):
+        if hop:
+            add(hop, 0, False)
+        for turn in range(1, subs):
+            for step in range(count):
+                to_sub(hop, turn, step).wait_recv()
+            add(hop, turn, False)
+    update[...] = (gate[...] * total[...]).astype(update.dtype)
+    for step in range(count):
+        if step:
+            to_seq(step).wait_send()
+        for hop in range(1, heads):
+            to_head(hop, step).wait_send()
+        for hop in range(heads):
+            for turn in range(1, subs):
+                to_sub(hop, turn, step).wait_send()
+
+
+def spread(own, w_all, gate):
+    count, heads, subs = (lax.axis_size(axis) for axis in ("seq", "head", "sub"))
+    rows, size = own.shape[1:]
+    vmem = pl.BlockSpec(memory_space=pltpu.VMEM)
+    dma = pltpu.SemaphoreType.DMA
+    return pl.pallas_call(
+        functools.partial(spread_kernel, count, heads, subs),
+        out_shape=jax.ShapeDtypeStruct((rows, w_all.shape[-1]), jnp.bfloat16),
+        in_specs=[vmem] * 3,
+        out_specs=vmem,
+        scratch_shapes=[
+            pltpu.VMEM((heads, subs, rows, count * size), jnp.bfloat16),
+            pltpu.VMEM((rows, w_all.shape[-1]), jnp.float32),
+            dma((2, count)),
+            dma((heads, 2, count)),
+            dma((heads, subs, 2, count)),
+            dma,
+        ],
+        compiler_params=pltpu.CompilerParams(
+            collective_id=3, has_side_effects=True, vmem_limit_bytes=40 * 1024 * 1024
+        ),
+        name="spread",
+    )(own, w_all, gate)
+
+
+def shards_by_head(tokens, modulation, w_qkv, w_out, pattern, counts, spatial_mask):
+    count = lax.axis_size("seq")
+    blocks = lax.axis_size("head") * lax.axis_size("sub")
+    row_count = tokens.shape[0]
+    depth, pairs_local, width = w_qkv.shape
+    quarter = row_count // blocks
+    place = lax.axis_index(("head", "sub"))
+    span = BLOCK // count
+    hid_own = modulate(lax.dynamic_slice_in_dim(tokens, place * quarter, quarter, 0), modulation)
+    w_parts = w_qkv.reshape(depth, count, width // 2).transpose(1, 0, 2)
+    slot_total = pattern.shape[1]
+    entries = jnp.concatenate([pattern.reshape(-1), counts.reshape(-1), spatial_mask.reshape(-1)])
+    lists = jnp.pad(entries, (0, 8 * 128 - entries.shape[0])).reshape(8, 128)
+    heads_in, whole_out, lists_all = by_head(hid_own, w_parts, w_out, lists, span, BLOCK)
+    entries = lists_all.reshape(count, -1)
+    listed = pattern.shape[0] * slot_total
+    table = entries[:, :listed].reshape(-1, slot_total)
+    used = entries[:, listed : listed + counts.shape[0]].reshape(-1)
+    masked = entries[:, listed + counts.shape[0] :][:, : spatial_mask.size].reshape(-1, slot_total)
+    order = jnp.arange(slot_total, dtype=jnp.int32)
+    query = jnp.arange(table.shape[0], dtype=jnp.int32)
+    frame_blocks = (query // slot_total * slot_total)[:, None] + order[None, :]
+    role = lax.rem(lax.axis_index("seq"), 2)
+    index = jnp.where(role == 0, table, frame_blocks)
+    alive = jnp.where(role == 0, order[None, :] < used[:, None], masked > 0).astype(jnp.float32)
+    own = attend(role[None], index, alive, heads_in, count, span)
+    out_width = w_out.shape[1]
+    gate_slice = lax.dynamic_slice_in_dim(modulation[2], place * out_width, out_width, 0)
+    return spread(own, whole_out.reshape(blocks, -1, out_width), gate_slice[None, :])
+
+
+def one_head_each(mesh_count, blocks, tokens, w_qkv, pattern, spatial_mask):
+    rows, frames = tokens.shape[0], spatial_mask.shape[0]
+    return (
+        w_qkv.shape[1] * 2 == mesh_count > 2
+        and frames == 1
+        and spatial_mask.shape[2] == pattern.shape[1]
+        and rows == BLOCK * spatial_mask.shape[1]
+        and BLOCK % (16 * mesh_count) == 0
+        and w_qkv.shape[0] % 128 == 0
+        and rows % (16 * blocks) == 0
+    )
+
+
+def shards_any(*args):
+    tokens, _, w_qkv, _, pattern, _, spatial_mask = args
+    blocks = lax.axis_size("head") * lax.axis_size("sub")
+    if one_head_each(lax.axis_size("seq"), blocks, tokens, w_qkv, pattern, spatial_mask):
+        return shards_by_head(*args)
+    return shards(*args)
+
 
 def solution(mesh):
     return jax.shard_map(
-        shards,
+        shards_any,
         mesh=mesh,
         in_specs=(
             P(("groups", "seq"), None),

time: 214 us -> 170 us (0.79)
  starting transfers between devices: 16 us -> 0 us
  waiting for transfers between devices: 15.8 us -> 0 us
  local copies, waits for them, and re-layouts: 25.9 us -> 15.9 us
  matrix products: 7.66 us -> 0 us
  Pallas kernels: 137 us -> 144 us
    all_to_all x2 -> x0, waiting for transfers between devices: 15.5 us -> none  [the longest x1 14.4 us: shards(): lax.all_to_all(temporal_in, 'seq', split_axis=0, concat_axis=1, tiled=True)]
    all_to_all x2 -> x0, starting transfers between devices: 10 us -> none  [the longest x1 5.48 us: shards(): lax.all_to_all(outcome, 'seq', split_axis=1, concat_axis=0, tiled=True)]
    dot_general x10 -> x0, matrix products: 7.66 us -> none  [the longest x1 3.08 us: shards(): jnp.einsum('fnpq,fqnc->fpnc', weights.astype(jnp.bfloat16), spatial[...,...]
    pallas_call x2 -> x3, Pallas kernels: 137 us -> 144 us  [the longest x1 112 us: by_head(): pl.pallas_call(functools.partial(by_head_kernel, sizes, chunks, o_chunks,...]
    ppermute x2 -> x0, starting transfers between devices: 5.98 us -> none  [the longest x1 4.7 us: with_halo(): lax.ppermute(head, axis, [((i + 1) % count, i) for i in range(ends)])]
    reshape x5, local copies, waits for them, and re-layouts: 9.58 us -> 4.6 us  [the longest x1 2.99 us: shards_by_head(): w_parts = w_qkv.reshape(depth, count, width // 2).transpose(1, 0, 2)]
    unnamed x32 -> x15, local copies, waits for them, and re-layouts: 6.71 us -> 11 us
    transpose x2 -> x0, local copies, waits for them, and re-layouts: 2.47 us -> none  [the longest x1 1.42 us: shards(): temporal_in = packed[..., :3 * head_size].transpose(1, 0, 2, 3)]
  transfers between devices with their start and end apart: 4 -> 0, of which waited for: 3 -> 0; matrix products, arithmetic and copies ran while one was open for 3% -> 0% of each run, Pallas kernels for 0% -> 0%
where the time goes in v2:
time: 170 us; the launch traced here: 166 us
  Pallas kernels  144 us (85%)
  local copies, waits for them, and re-layouts  15.9 us (9%)
  other arithmetic  6.68 us (4%)
    pallas_call x1, Pallas kernels, by_head(): pl.pallas_call(functools.partial(by_head_kernel, sizes, chunks, o_chunks,...  112 us
    pallas_call x1, Pallas kernels, spread(): pl.pallas_call(functools.partial(spread_kernel, count, heads, subs), out_...  23.6 us
    unnamed x15, local copies, waits for them, and re-layouts  11 us
    pallas_call x1, Pallas kernels, attend(): pl.pallas_call(functools.partial(attend_kernel, count, span, 1.0 / math.s...  8.32 us

profile of v2, /device:TPU:25, one launch (start us, length us, event | category | flops | bytes accessed | tf_op | source)
XLA Modules:
  0.0 166.4 jit_solution(1353699891661544644)
XLA Ops:
  0.0 0.0 copy-start.5
  0.0 0.8 reshape.51
  0.8 0.8 reshape.52
  1.5 0.7 pad_add_fusion
  2.3 0.0 copy-start.4
  2.3 1.5 convert_reduce_fusion
  3.8 1.5 fusion.2
  5.3 0.0 copy-done.5
  5.3 1.5 fusion.5.hid_own
  6.9 0.0 copy-done.4
  6.9 4.9 %copy.8 = bf16[768,2,768]{0,2,1:T(8,128)(2,1)} copy(bf16[768,2,768]{2,1,0:T(2,128)(2,1)S(1)} %copy-done.4) | data formatting | bytes 4718592 | tf_op args[2]
  11.8 3.0 %copy.9 = bf16[768,4,384]{2,0,1:T(8,128)(2,1)S(1)} copy(bf16[768,4,384]{0,2,1:T(8,128)(2,1)} %bitcast.13) | data formatting | bytes 4718592 | tf_op jit(solution)/shard_map/reshape | solution.py:892
  14.8 0.0 copy-start.3
  14.8 1.1 copy-done.3
  15.9 111.8 %by_head.1 = (bf16[16,128,384]{2,1,0:T(8,128)(2,1)S(1)}, bf16[4,512,768]{2,1,0:T(8,128)(2,1)}, s32[4,8,128]{2,1,0:T(8,128)S(1)}) custom-call(bf16[128,3072]{1,0:T(8,128)(2,1)S(1)} %fusion.5.hid_own, bf16[4,768,384]{2,1,0:T(8,128)(2,1)S(1)} %bitcast.11, bf16[512,768]{1,0:T(8,128)(2,1)S(1)} %copy-done.3, s32[8,128]{1,0:T(8,128)S(1)} %pad_bitcast_fusion.lists), custom_call_target="tpu_custom_call" | custom-call | tf_op jit(solution)/shard_map/by_head/pallas_call | solution.py:695
  127.8 0.0 copy-start.2
  127.8 1.1 copy-done.2
  128.9 0.1 slice_compare_fusion
  129.0 0.1 gt.11
  129.1 0.1 slice.27
  129.1 0.1 lt.20
  129.2 0.7 fusion.7.alive
  129.9 0.1 reshape.55
  130.0 0.7 add_select_fusion.index
  130.7 8.3 %attend.1.own = bf16[4,512,128]{2,1,0:T(8,128)(2,1)} custom-call(s32[1]{0:T(128)} %bitcast.role, s32[16,4]{1,0:T(8,128)} %add_select_fusion.index, f32[16,4]{1,0:T(8,128)} %fusion.7.alive, bf16[16,128,384]{2,1,0:T(8,128)(2,1)} %copy-done.2), custom_call_target="tpu_custom_call" | custom-call | tf_op jit(solution)/shard_map/attend/pallas_call | solution.py:767
  139.0 0.0 copy-start
  139.0 1.9 %copy-done = bf16[4,512,768]{2,1,0:T(8,128)(2,1)S(1)} copy-done((bf16[4,512,768]{2,1,0:T(8,128)(2,1)S(1)}, bf16[4,512,768]{2,1,0:T(8,128)(2,1)}, u32[]{:S(2)}) %copy-start) | copy-done | bytes 3145752
  140.9 0.0 copy-start.1
  140.9 1.0 copy-done.1
  141.9 23.6 %spread.1 = bf16[512,768]{1,0:T(8,128)(2,1)S(1)} custom-call(bf16[4,512,128]{2,1,0:T(8,128)(2,1)S(1)} %copy-done.1, bf16[4,512,768]{2,1,0:T(8,128)(2,1)S(1)} %copy-done, f32[1,768]{1,0:T(1,128)S(1)} %constant_dynamic-slice_fusion.gate), custom_call_target="tpu_custom_call" | custom-call | tf_op jit(solution)/shard_map/spread/pallas_call | solution.py:863
  165.6 0.9 copy.14
  (8 shorter events, 0.1 us)
Async XLA Ops:
  0.0 5.3 %copy-start.5 = (f32[3,3072]{1,0:T(4,128)S(1)}, f32[3,3072]{1,0:T(4,128)}, u32[]{:S(2)}) copy-start(f32[3,3072]{1,0:T(4,128)} %param.8) | copy-start | bytes 110596
  2.3 4.6 %copy-start.4 = (bf16[768,2,768]{2,1,0:T(2,128)(2,1)S(1)}, bf16[768,2,768]{2,1,0:T(2,128)(2,1)}, u32[]{:S(2)}) copy-start(bf16[768,2,768]{2,1,0:T(2,128)(2,1)} %param.9) | copy-start | bytes 7077892
  14.8 1.1 copy-start.3
  127.8 1.2 copy-start.2
  139.0 1.9 %copy-start = (bf16[4,512,768]{2,1,0:T(8,128)(2,1)S(1)}, bf16[4,512,768]{2,1,0:T(8,128)(2,1)}, u32[]{:S(2)}) copy-start(bf16[4,512,768]{2,1,0:T(8,128)(2,1)} %get-tuple-element.10.w_all) | copy-start | bytes 9437188
  140.9 1.0 copy-start.1

commit v3 on v2

--- a/solution.py
+++ b/solution.py
@@ -471,8 +471,9 @@
 
 
 def by_head_kernel(
-    sizes, chunks, o_chunks, span, hid_own, w_parts, o_own, lists, blocks, o_all, lists_all,
-    hfull, wfull, w_sems, l_sems, z_sems, x_sems, c_sems, o_sems, own_sems,
+    sizes, chunks, o_chunks, span, hid_own, w_own, o_own, lists, gate, update,
+    hfull, wfull, blocks, o_all, lists_all, table, own, slots, total,
+    w_sems, l_sems, z_sems, x_sems, c_sems, o_sems, own_sems, sz_sems, sx_sems, sc_sems,
 ):
     count, parts, heads, subs = sizes
     me, group = lax.axis_index("seq"), lax.axis_index("groups")
@@ -480,7 +481,8 @@
     meet(("seq", "groups", "head", "sub"))
     quarter = hid_own.shape[0]
     size = quarter // chunks
-    half = w_parts.shape[1] // parts
+    half = w_own.shape[0] // parts
+    width = wfull.shape[2]
     mine = pl.ds(pl.multiple_of(group * half, half), half)
 
     def place(hop, axis, size_):
@@ -489,9 +491,12 @@
     def source_of(hop):
         return lax.rem(me + count - hop, count)
 
+    def w_part(other):
+        return pl.ds(pl.multiple_of(other * width, width), width)
+
     def w_along(hop, shard):
         return push(
-            w_parts.at[place(hop, "seq", count), mine], wfull.at[shard, mine],
+            w_own.at[mine, w_part(place(hop, "seq", count))], wfull.at[shard, mine],
             w_sems.at[0, 0, hop], w_sems.at[0, 1, hop], "seq", place(hop, "seq", count),
         )
 
@@ -558,7 +563,7 @@
             c_push(me, chunk, 0, turn, True).start()
     keeps = [
         pltpu.make_async_copy(o_own, o_all.at[me], own_sems.at[0]),
-        pltpu.make_async_copy(w_parts.at[me], wfull.at[me], own_sems.at[1]),
+        pltpu.make_async_copy(w_own.at[:, w_part(me)], wfull.at[me], own_sems.at[1]),
         pltpu.make_async_copy(
             hid_own,
             hfull.at[me, pl.ds(pl.multiple_of((head * subs + sub) * quarter, quarter), quarter)],
@@ -649,11 +654,19 @@
     finish(count - 2)
     x_relay(count - 1)
     finish(count - 1)
-    for step in range(2, count):
-        outs.relay(step)
-
     for hop in range(1, count):
         l_along(hop).wait_recv()
+    to_table = pltpu.make_async_copy(lists_all, table, own_sems.at[4])
+    to_table.start()
+    to_table.wait()
+    scale = 1.0 / math.sqrt(own.shape[2])
+    attend(count, span, scale, lax.rem(me, 2), table, blocks, own)
+    spread(
+        count, heads, subs, outs, own, o_all, gate, update, slots, total,
+        sz_sems, sx_sems, sc_sems, own_sems.at[5],
+    )
+
+    for hop in range(1, count):
         l_along(hop).wait_send()
         w_along(hop, me).wait_send()
         for turn in range(1, parts):
@@ -676,66 +689,73 @@
                             c_push(shard, chunk, hop, turn).wait_send()
     for step in range(1, count):
         outs.close_sends(step)
-        for way in (0, 1):
-            @pl.when(outs.present(step, way))
-            def _():
-                outs.complete(outs.shard_of(step, way))
     outs.close_own()
 
 
-def by_head(hid_own, w_parts, o_own, lists, span, block):
+def by_head(hid_own, w_own, o_own, lists, gate, span, block):
     sizes = tuple(lax.axis_size(axis) for axis in ("seq", "groups", "head", "sub"))
     count, parts, heads, subs = sizes
     rows = hid_own.shape[0] * heads * subs
-    depth, width = hid_own.shape[1], w_parts.shape[2]
+    depth, width = hid_own.shape[1], w_own.shape[1] // count
     chunks = pieces_of(hid_own.shape[0], 2)
     o_chunks = pieces_of(o_own.shape[0] // parts, 2)
     vmem = pl.BlockSpec(memory_space=pltpu.VMEM)
     dma = pltpu.SemaphoreType.DMA
     return pl.pallas_call(
         functools.partial(by_head_kernel, sizes, chunks, o_chunks, span),
-        out_shape=[
-            jax.ShapeDtypeStruct((count * rows // block, block, width), jnp.bfloat16),
-            jax.ShapeDtypeStruct((count,) + o_own.shape, jnp.bfloat16),
-            jax.ShapeDtypeStruct((count,) + lists.shape, lists.dtype),
-        ],
-        in_specs=[vmem] * 4,
-        out_specs=[vmem, pl.BlockSpec(memory_space=pl.ANY), vmem],
+        out_shape=jax.ShapeDtypeStruct((rows, o_own.shape[1]), jnp.bfloat16),
+        in_specs=[vmem] * 5,
+        out_specs=vmem,
         scratch_shapes=[
             pltpu.VMEM((count, rows, depth), jnp.bfloat16),
-            pltpu.VMEM((count,) + w_parts.shape[1:], jnp.bfloat16),
+            pltpu.VMEM((count, w_own.shape[0], width), jnp.bfloat16),
+            pltpu.VMEM((count * rows // block, block, width), jnp.bfloat16),
+            pltpu.VMEM((count,) + o_own.shape, jnp.bfloat16),
+            pltpu.VMEM((count,) + lists.shape, lists.dtype),
+            pltpu.SMEM((count,) + lists.shape, lists.dtype),
+            pltpu.VMEM((count, rows, width // 3), jnp.bfloat16),
+            pltpu.VMEM((heads, subs, rows, count * width // 3), jnp.bfloat16),
+            pltpu.VMEM((rows, o_own.shape[1]), jnp.float32),
             dma((parts, 2, count)),
             dma((2, count)),
             dma((2, 2, count, chunks)),
             dma((heads, 2, count, chunks)),
             dma((heads, subs, 2, count, chunks)),
             dma((1 + parts, 2, count, o_chunks)),
-            dma((4,)),
+            dma((6,)),
+            dma((2, count)),
+            dma((heads, 2, count)),
+            dma((heads, subs, 2, count)),
         ],
         compiler_params=pltpu.CompilerParams(
-            collective_id=2, has_side_effects=True, vmem_limit_bytes=48 * 1024 * 1024
+            collective_id=2, has_side_effects=True, vmem_limit_bytes=56 * 1024 * 1024
         ),
         name="by_head",
-    )(hid_own, w_parts, o_own, lists)
-
-
-def attend_kernel(count, span, scale, role, index, alive, blocks, out):
+    )(hid_own, w_own, o_own, lists, gate)
+
+
+def attend(count, span, scale, role, table, blocks, out):
     total, block, width = blocks.shape
     size = width // 3
-    slots = index.shape[1]
     each = total // count
+    slots = each
 
     def query(b, carry):
+        device, row = b // each, lax.rem(b, each)
+        used = table[device, 0, each * slots + row]
         q = blocks[b, :, :size]
         numerator = jnp.zeros((block, size), jnp.float32)
         denominator = jnp.zeros((block, 1), jnp.float32)
         for j in range(slots):
-            at = index[b, j]
+            listed = table[device, 0, row * slots + j]
+            seen = table[device, 0, each * (slots + 1) + row * slots + j]
+            at = jnp.where(role == 0, listed, device * each + j)
+            alive = jnp.where(role == 0, jnp.where(j < used, 1.0, 0.0), jnp.where(seen > 0, 1.0, 0.0))
             scores = lax.dot_general(
                 q, blocks[at, :, size : 2 * size], (((1,), (1,)), ((), ())),
                 preferred_element_type=jnp.float32,
             )
-            weights = jnp.exp(scores * scale) * alive[b, j]
+            weights = jnp.exp(scores * scale) * alive
             denominator = denominator + jnp.sum(weights, axis=-1, keepdims=True)
             numerator = numerator + jnp.dot(
                 weights.astype(jnp.bfloat16), blocks[at, :, 2 * size :],
@@ -743,41 +763,25 @@
             )
         result = (numerator / denominator).astype(out.dtype)
 
-        @pl.when(role[0] == 0)
+        @pl.when(role == 0)
         def _():
             at = pl.ds(pl.multiple_of(b * span, span), span)
             for f in range(count):
                 out[f, at, :] = result[f * span : (f + 1) * span]
 
-        @pl.when(role[0] == 1)
+        @pl.when(role == 1)
         def _():
-            at = pl.ds(pl.multiple_of(lax.rem(b, each) * block, block), block)
-            out[b // each, at, :] = result
+            out[device, pl.ds(pl.multiple_of(row * block, block), block), :] = result
 
         return carry
 
     lax.fori_loop(0, total, query, 0, unroll=2)
 
 
-def attend(role, index, alive, blocks, count, span):
-    total, block, width = blocks.shape
-    size = width // 3
-    smem = pl.BlockSpec(memory_space=pltpu.SMEM)
-    vmem = pl.BlockSpec(memory_space=pltpu.VMEM)
-    return pl.pallas_call(
-        functools.partial(attend_kernel, count, span, 1.0 / math.sqrt(size)),
-        out_shape=jax.ShapeDtypeStruct((count, total * block // count, size), jnp.bfloat16),
-        in_specs=[smem, smem, smem, vmem],
-        out_specs=vmem,
-        name="attend",
-    )(role, index, alive, blocks)
-
-
-def spread_kernel(
-    count, heads, subs, own, w_all, gate, update, slots, total, z_sems, x_sems, c_sems, own_sem
+def spread(
+    count, heads, subs, outs, own, w_all, gate, update, slots, total, z_sems, x_sems, c_sems, own_sem
 ):
     me, head, sub = (lax.axis_index(axis) for axis in ("seq", "head", "sub"))
-    meet(("seq", "head", "sub"))
     size = own.shape[2]
 
     def columns(step):
@@ -825,6 +829,8 @@
     keep = pltpu.make_async_copy(own.at[me], spot(0, 0, 0), own_sem)
     keep.start()
     for step in range(1, count):
+        if step > 1:
+            outs.relay(step)
         to_seq(step).wait_recv()
         hand_over(step)
         pass_on(step - 1)
@@ -835,8 +841,13 @@
         product = jnp.dot(slots[hop, turn], w_all[owner], preferred_element_type=jnp.float32)
         total[...] = product if first else total[...] + product
 
+    pass_on(count - 1)
+    for step in range(1, count):
+        for way in (0, 1):
+            @pl.when(outs.present(step, way))
+            def _():
+                outs.complete(outs.shard_of(step, way))
     add(0, 0, True)
-    pass_on(count - 1)
     for hop in range(heads):
         if hop:
             add(hop, 0, False)
@@ -855,60 +866,22 @@
                 to_sub(hop, turn, step).wait_send()
 
 
-def spread(own, w_all, gate):
-    count, heads, subs = (lax.axis_size(axis) for axis in ("seq", "head", "sub"))
-    rows, size = own.shape[1:]
-    vmem = pl.BlockSpec(memory_space=pltpu.VMEM)
-    dma = pltpu.SemaphoreType.DMA
-    return pl.pallas_call(
-        functools.partial(spread_kernel, count, heads, subs),
-        out_shape=jax.ShapeDtypeStruct((rows, w_all.shape[-1]), jnp.bfloat16),
-        in_specs=[vmem] * 3,
-        out_specs=vmem,
-        scratch_shapes=[
-            pltpu.VMEM((heads, subs, rows, count * size), jnp.bfloat16),
-            pltpu.VMEM((rows, w_all.shape[-1]), jnp.float32),
-            dma((2, count)),
-            dma((heads, 2, count)),
-            dma((heads, subs, 2, count)),
-            dma,
-        ],
-        compiler_params=pltpu.CompilerParams(
-            collective_id=3, has_side_effects=True, vmem_limit_bytes=40 * 1024 * 1024
-        ),
-        name="spread",
-    )(own, w_all, gate)
-
-
 def shards_by_head(tokens, modulation, w_qkv, w_out, pattern, counts, spatial_mask):
     count = lax.axis_size("seq")
     blocks = lax.axis_size("head") * lax.axis_size("sub")
     row_count = tokens.shape[0]
-    depth, pairs_local, width = w_qkv.shape
+    depth = w_qkv.shape[0]
     quarter = row_count // blocks
     place = lax.axis_index(("head", "sub"))
     span = BLOCK // count
     hid_own = modulate(lax.dynamic_slice_in_dim(tokens, place * quarter, quarter, 0), modulation)
-    w_parts = w_qkv.reshape(depth, count, width // 2).transpose(1, 0, 2)
-    slot_total = pattern.shape[1]
     entries = jnp.concatenate([pattern.reshape(-1), counts.reshape(-1), spatial_mask.reshape(-1)])
     lists = jnp.pad(entries, (0, 8 * 128 - entries.shape[0])).reshape(8, 128)
-    heads_in, whole_out, lists_all = by_head(hid_own, w_parts, w_out, lists, span, BLOCK)
-    entries = lists_all.reshape(count, -1)
-    listed = pattern.shape[0] * slot_total
-    table = entries[:, :listed].reshape(-1, slot_total)
-    used = entries[:, listed : listed + counts.shape[0]].reshape(-1)
-    masked = entries[:, listed + counts.shape[0] :][:, : spatial_mask.size].reshape(-1, slot_total)
-    order = jnp.arange(slot_total, dtype=jnp.int32)
-    query = jnp.arange(table.shape[0], dtype=jnp.int32)
-    frame_blocks = (query // slot_total * slot_total)[:, None] + order[None, :]
-    role = lax.rem(lax.axis_index("seq"), 2)
-    index = jnp.where(role == 0, table, frame_blocks)
-    alive = jnp.where(role == 0, order[None, :] < used[:, None], masked > 0).astype(jnp.float32)
-    own = attend(role[None], index, alive, heads_in, count, span)
     out_width = w_out.shape[1]
     gate_slice = lax.dynamic_slice_in_dim(modulation[2], place * out_width, out_width, 0)
-    return spread(own, whole_out.reshape(blocks, -1, out_width), gate_slice[None, :])
+    return by_head(
+        hid_own, w_qkv.reshape(depth, -1), w_out, lists, gate_slice[None, :], span, BLOCK
+    )
 
 
 def one_head_each(mesh_count, blocks, tokens, w_qkv, pattern, spatial_mask):
@@ -916,6 +889,9 @@
     return (
         w_qkv.shape[1] * 2 == mesh_count > 2
         and frames == 1
+        and mesh_count == blocks
+        and pattern.shape[0] == pattern.shape[1] == spatial_mask.shape[1]
+        and 2 * pattern.size + pattern.shape[0] <= 128
         and spatial_mask.shape[2] == pattern.shape[1]
         and rows == BLOCK * spatial_mask.shape[1]
         and BLOCK % (16 * mesh_count) == 0

time: 170 us -> 148 us (0.87); the launches traced: 166 us -> 148 us
  local copies, waits for them, and re-layouts: 15.9 us -> 6.65 us
  Pallas kernels: 144 us -> 135 us
    pallas_call x2 -> x0, Pallas kernels: 32 us -> none  [the longest x1 23.6 us: spread(): pl.pallas_call(functools.partial(spread_kernel, count, heads, subs), out_...]
    pallas_call x1, Pallas kernels: 112 us -> 135 us  [by_head(): pl.pallas_call(functools.partial(by_head_kernel, sizes, chunks, o_chunks,...]
    unnamed x15 -> x6, local copies, waits for them, and re-layouts: 11 us -> 3.92 us
    reshape x2 -> x0, local copies, waits for them, and re-layouts: 3.06 us -> none  [the longest x1 2.99 us: shards_by_head(): w_parts = w_qkv.reshape(depth, count, width // 2).transpose(1, 0, 2)]
where the time goes in v3:
time: 148 us
  Pallas kernels  135 us (91%)
  local copies, waits for them, and re-layouts  6.65 us (4%)
  other arithmetic  6.14 us (4%)
    pallas_call x1, Pallas kernels, by_head(): pl.pallas_call(functools.partial(by_head_kernel, sizes, chunks, o_chunks,...  135 us
    unnamed x6, local copies, waits for them, and re-layouts  3.92 us

profile of v3, /device:TPU:25, one launch (start us, length us, event | category | flops | bytes accessed | tf_op | source)
XLA Modules:
  0.0 148.0 jit_solution(2184275635658554145)
XLA Ops:
  0.0 0.0 copy-start.1
  0.0 0.8 reshape.27
  0.8 0.8 reshape.28
  1.5 0.7 pad_add_fusion
  2.3 0.0 copy-start
  2.3 1.5 convert_reduce_fusion
  3.8 1.5 %fusion.2 = f32[128]{0:T(128)S(1)} fusion(f32[128]{0:T(128)S(1)} %broadcast_multiply_fusion, bf16[512,3072]{1,0:T(8,128)(2,1)} %param.7, s32[]{:T(128)S(6)} %select_n.6), kind=kLoop, calls=%fused_computation.4 | loop fusion | flops 1572736 | bytes 787460 | tf_op jit(solution)/shard_map/reduce_sum | solution.py:357
  5.3 0.6 pad_bitcast_fusion.lists
  5.9 0.0 copy-done.1
  5.9 0.6 constant_dynamic-slice_fusion.gate
  6.5 2.4 %fusion.5.hid_own = bf16[128,3072]{1,0:T(8,128)(2,1)} fusion(f32[3072]{0:T(1024)S(1)} %bitcast.9, f32[3072]{0:T(1024)S(1)} %bitcast.8, f32[128]{0:T(128)S(1)} %add_rsqrt_fusion, f32[128]{0:T(128)S(1)} %broadcast_multiply_fusion, bf16[512,3072]{1,0:T(8,128)(2,1)} %param.7, s32[]{:T(128)S(6)} %select_n.6), kind=kLoop, calls=%fused_computation.7 | loop fusion | flops 2359296 | bytes 1598468 | tf_op jit(solution)/shard_map/convert_element_type | solution.py:359
  8.9 0.0 copy-done
  8.9 1.8 %copy.8 = bf16[96,8,2,768]{3,1,2,0:T(8,128)(2,1)} copy(bf16[96,8,2,768]{3,2,1,0:T(2,128)(2,1)S(1)} %bitcast.7) | data formatting | bytes 4718592
  10.7 135.2 %by_head.1 = bf16[512,768]{1,0:T(8,128)(2,1)} custom-call(bf16[128,3072]{1,0:T(8,128)(2,1)} %fusion.5.hid_own, bf16[768,1536]{1,0:T(8,128)(2,1)} %bitcast.6, bf16[512,768]{1,0:T(8,128)(2,1)} %o_own.1, s32[8,128]{1,0:T(8,128)} %pad_bitcast_fusion.lists, f32[1,768]{1,0:T(1,128)} %constant_dynamic-slice_fusion.gate), custom_call_target="tpu_custom_call" | custom-call | tf_op jit(solution)/shard_map/by_head/pallas_call | solution.py:704
  145.9 2.1 %copy.10 = bf16[512,768]{1,0:T(8,128)(2,1)} copy(bf16[512,768]{1,0:T(8,128)(2,1)} %by_head.1) | data formatting | bytes 1572864
  (3 shorter events, 0.0 us)
Async XLA Ops:
  0.0 5.9 %copy-start.1 = (f32[3,3072]{1,0:T(4,128)S(1)}, f32[3,3072]{1,0:T(4,128)}, u32[]{:S(2)}) copy-start(f32[3,3072]{1,0:T(4,128)} %param.8) | copy-start | bytes 110596
  2.3 6.6 %copy-start = (bf16[768,2,768]{2,1,0:T(2,128)(2,1)S(1)}, bf16[768,2,768]{2,1,0:T(2,128)(2,1)}, u32[]{:S(2)}) copy-start(bf16[768,2,768]{2,1,0:T(2,128)(2,1)} %param.9) | copy-start | bytes 7077892

commit v4 on v3

--- a/solution.py
+++ b/solution.py
@@ -650,10 +650,10 @@
             x_relay(step - 2)
             finish(step - 2)
     x_relay(count - 2)
-    outs.relay(1)
     finish(count - 2)
     x_relay(count - 1)
     finish(count - 1)
+    outs.relay(1)
     for hop in range(1, count):
         l_along(hop).wait_recv()
     to_table = pltpu.make_async_copy(lists_all, table, own_sems.at[4])
@@ -697,7 +697,7 @@
     count, parts, heads, subs = sizes
     rows = hid_own.shape[0] * heads * subs
     depth, width = hid_own.shape[1], w_own.shape[1] // count
-    chunks = pieces_of(hid_own.shape[0], 2)
+    chunks = pieces_of(hid_own.shape[0], 4)
     o_chunks = pieces_of(o_own.shape[0] // parts, 2)
     vmem = pl.BlockSpec(memory_space=pltpu.VMEM)
     dma = pltpu.SemaphoreType.DMA
@@ -742,13 +742,13 @@
 
     def query(b, carry):
         device, row = b // each, lax.rem(b, each)
-        used = table[device, 0, each * slots + row]
+        used = table[device, each, row]
         q = blocks[b, :, :size]
         numerator = jnp.zeros((block, size), jnp.float32)
         denominator = jnp.zeros((block, 1), jnp.float32)
         for j in range(slots):
-            listed = table[device, 0, row * slots + j]
-            seen = table[device, 0, each * (slots + 1) + row * slots + j]
+            listed = table[device, row, j]
+            seen = table[device, row, slots + j]
             at = jnp.where(role == 0, listed, device * each + j)
             alive = jnp.where(role == 0, jnp.where(j < used, 1.0, 0.0), jnp.where(seen > 0, 1.0, 0.0))
             scores = lax.dot_general(
@@ -866,6 +866,40 @@
                 to_sub(hop, turn, step).wait_send()
 
 
+def modulate_kernel(tokens, modulation, hidden, held, sem):
+    quarter = held.shape[0]
+    place = lax.axis_index("head") * lax.axis_size("sub") + lax.axis_index("sub")
+    rows = pl.ds(pl.multiple_of(place * quarter, quarter), quarter)
+    fetch = pltpu.make_async_copy(tokens.at[rows], held, sem)
+    fetch.start()
+    fetch.wait()
+    gain = 1.0 + modulation[1:2, :]
+    shift = modulation[0:1, :]
+
+    def some(i, carry):
+        at = pl.ds(pl.multiple_of(i * 16, 16), 16)
+        values = held[at, :].astype(jnp.float32)
+        centered = values - jnp.mean(values, axis=-1, keepdims=True)
+        spread_of = jnp.mean(jnp.square(centered), axis=-1, keepdims=True)
+        normed = centered * lax.rsqrt(spread_of + EPSILON)
+        hidden[at, :] = (normed * gain + shift).astype(hidden.dtype)
+        return carry
+
+    lax.fori_loop(0, quarter // 16, some, 0)
+
+
+def modulate_part(tokens, modulation, quarter):
+    vmem = pl.BlockSpec(memory_space=pltpu.VMEM)
+    return pl.pallas_call(
+        modulate_kernel,
+        out_shape=jax.ShapeDtypeStruct((quarter, tokens.shape[1]), tokens.dtype),
+        in_specs=[pl.BlockSpec(memory_space=pl.ANY), vmem],
+        out_specs=vmem,
+        scratch_shapes=[pltpu.VMEM((quarter, tokens.shape[1]), tokens.dtype), pltpu.SemaphoreType.DMA],
+        name="modulate_part",
+    )(tokens, modulation)
+
+
 def shards_by_head(tokens, modulation, w_qkv, w_out, pattern, counts, spatial_mask):
     count = lax.axis_size("seq")
     blocks = lax.axis_size("head") * lax.axis_size("sub")
@@ -874,9 +908,13 @@
     quarter = row_count // blocks
     place = lax.axis_index(("head", "sub"))
     span = BLOCK // count
-    hid_own = modulate(lax.dynamic_slice_in_dim(tokens, place * quarter, quarter, 0), modulation)
-    entries = jnp.concatenate([pattern.reshape(-1), counts.reshape(-1), spatial_mask.reshape(-1)])
-    lists = jnp.pad(entries, (0, 8 * 128 - entries.shape[0])).reshape(8, 128)
+    hid_own = modulate_part(tokens, modulation, quarter)
+    each = counts.shape[0]
+    lists = (
+        jnp.pad(pattern, ((0, 8 - each), (0, 128 - each)))
+        + jnp.pad(counts[None, :], ((each, 7 - each), (0, 128 - each)))
+        + jnp.pad(spatial_mask[0], ((0, 8 - each), (each, 128 - 2 * each)))
+    )
     out_width = w_out.shape[1]
     gate_slice = lax.dynamic_slice_in_dim(modulation[2], place * out_width, out_width, 0)
     return by_head(
@@ -891,7 +929,7 @@
         and frames == 1
         and mesh_count == blocks
         and pattern.shape[0] == pattern.shape[1] == spatial_mask.shape[1]
-        and 2 * pattern.size + pattern.shape[0] <= 128
+        and pattern.shape[0] < 8
         and spatial_mask.shape[2] == pattern.shape[1]
         and rows == BLOCK * spatial_mask.shape[1]
         and BLOCK % (16 * mesh_count) == 0

time: 148 us -> 147 us (level)
  Pallas kernels: 135 us -> 140 us
  other arithmetic: 6.14 us -> 1.52 us
    pallas_call x0 -> x1, Pallas kernels: none -> 4.81 us  [modulate_part(): pl.pallas_call(modulate_kernel, out_shape=jax.ShapeDtypeStruct((quarter,...]
    reduce_sum x2 -> x0, other arithmetic: 2.97 us -> none  [the longest x1 1.49 us: modulate(): spread = jnp.mean(jnp.square(values - center), axis=-1, keepdims=True)]
    convert_element_type x1 -> x0, other arithmetic: 2.4 us -> none  [modulate(): return (normed * (1.0 + modulation[1]) + modulation[0]).astype(jnp.bfloat16)]
    reshape x3 -> x0, local copies, waits for them, and re-layouts: 2.14 us -> none  [the longest x1 0.77 us: shards_by_head(): pattern.reshape(-1)]
    add x0 -> x1, other arithmetic: none -> 1.52 us  [shards_by_head(): jnp.pad(pattern, ((0, 8 - each), (0, 128 - each)))]
    unnamed x6 -> x4, local copies, waits for them, and re-layouts: 3.92 us -> 3.91 us
where the time goes in v4:
time: 147 us
  Pallas kernels  140 us (95%)
  local copies, waits for them, and re-layouts  5.33 us (4%)
  other arithmetic  1.52 us (1%)
    pallas_call x1, Pallas kernels, by_head(): pl.pallas_call(functools.partial(by_head_kernel, sizes, chunks, o_chunks,...  135 us
    pallas_call x1, Pallas kernels, modulate_part(): pl.pallas_call(modulate_kernel, out_shape=jax.ShapeDtypeStruct((quarter,...  4.81 us
    unnamed x4, local copies, waits for them, and re-layouts  3.91 us

profile of v4, /device:TPU:25, one launch (start us, length us, event | category | flops | bytes accessed | tf_op | source)
XLA Modules:
  0.0 146.6 jit_solution(12884911169322998346)
XLA Ops:
  0.0 0.0 copy-start
  0.0 1.5 %pad_add_fusion.lists = s32[8,128]{1,0:T(8,128)} fusion(s32[4,4]{1,0:T(4,128)} %bitcast.6, s32[1,4]{1,0:T(1,128)} %bitcast.7, s32[4,4]{1,0:T(4,128)} %param.11), kind=kLoop, calls=%fused_computation | loop fusion | flops 2048 | bytes 4240 | tf_op jit(solution)/shard_map/add | solution.py:914
  1.5 0.8 slice.3
  2.3 0.6 constant_dynamic-slice_fusion.gate
  2.9 4.8 %modulate_part.1.hid_own = bf16[128,3072]{1,0:T(8,128)(2,1)} custom-call(bf16[512,3072]{1,0:T(8,128)(2,1)} %tokens.1, f32[3,3072]{1,0:T(4,128)} %modulation.1), custom_call_target="tpu_custom_call" | custom-call | tf_op jit(solution)/shard_map/modulate_part/pallas_call | solution.py:893
  7.8 0.0 copy-done
  7.8 1.8 %copy.8 = bf16[96,8,2,768]{3,1,2,0:T(8,128)(2,1)} copy(bf16[96,8,2,768]{3,2,1,0:T(2,128)(2,1)S(1)} %bitcast.5) | data formatting | bytes 4718592
  9.6 134.9 %by_head.1 = bf16[512,768]{1,0:T(8,128)(2,1)} custom-call(bf16[128,3072]{1,0:T(8,128)(2,1)} %modulate_part.1.hid_own, bf16[768,1536]{1,0:T(8,128)(2,1)} %bitcast.4, bf16[512,768]{1,0:T(8,128)(2,1)} %o_own.1, s32[8,128]{1,0:T(8,128)} %pad_add_fusion.lists, f32[1,768]{1,0:T(1,128)} %constant_dynamic-slice_fusion.gate), custom_call_target="tpu_custom_call" | custom-call | tf_op jit(solution)/shard_map/by_head/pallas_call | solution.py:704
  144.5 2.1 %copy.10 = bf16[512,768]{1,0:T(8,128)(2,1)} copy(bf16[512,768]{1,0:T(8,128)(2,1)} %by_head.1) | data formatting | bytes 1572864
Async XLA Ops:
  0.0 7.8 %copy-start = (bf16[768,2,768]{2,1,0:T(2,128)(2,1)S(1)}, bf16[768,2,768]{2,1,0:T(2,128)(2,1)}, u32[]{:S(2)}) copy-start(bf16[768,2,768]{2,1,0:T(2,128)(2,1)} %param.9) | copy-start | bytes 7077892

commit v5 on v4

--- a/solution.py
+++ b/solution.py
@@ -885,7 +885,7 @@
         hidden[at, :] = (normed * gain + shift).astype(hidden.dtype)
         return carry
 
-    lax.fori_loop(0, quarter // 16, some, 0)
+    lax.fori_loop(0, quarter // 16, some, 0, unroll=4)
 
 
 def modulate_part(tokens, modulation, quarter):

time: 147 us -> 146 us (level)
  Pallas kernels: 140 us -> 138 us
where the time goes in v5:
time: 146 us; the launch traced here: 145 us
  Pallas kernels  138 us (95%)
  local copies, waits for them, and re-layouts  5.33 us (4%)
  other arithmetic  1.52 us (1%)
    pallas_call x1, Pallas kernels, by_head(): pl.pallas_call(functools.partial(by_head_kernel, sizes, chunks, o_chunks,...  135 us
    unnamed x4, local copies, waits for them, and re-layouts  3.91 us
    pallas_call x1, Pallas kernels, modulate_part(): pl.pallas_call(modulate_kernel, out_shape=jax.ShapeDtypeStruct((quarter,...  3.48 us

profile of v5, /device:TPU:25, one launch (start us, length us, event | category | flops | bytes accessed | tf_op | source)
XLA Modules:
  0.0 145.3 jit_solution(9022084067672620386)
XLA Ops:
  0.0 0.0 copy-start
  0.0 1.5 %pad_add_fusion.lists = s32[8,128]{1,0:T(8,128)} fusion(s32[4,4]{1,0:T(4,128)} %bitcast.6, s32[1,4]{1,0:T(1,128)} %bitcast.7, s32[4,4]{1,0:T(4,128)} %param.11), kind=kLoop, calls=%fused_computation | loop fusion | flops 2048 | bytes 4240 | tf_op jit(solution)/shard_map/add | solution.py:914
  1.5 0.8 slice.3
  2.3 0.6 constant_dynamic-slice_fusion.gate
  2.9 3.5 %modulate_part.1.hid_own = bf16[128,3072]{1,0:T(8,128)(2,1)} custom-call(bf16[512,3072]{1,0:T(8,128)(2,1)} %tokens.1, f32[3,3072]{1,0:T(4,128)} %modulation.1), custom_call_target="tpu_custom_call" | custom-call | tf_op jit(solution)/shard_map/modulate_part/pallas_call | solution.py:893
  6.4 0.0 copy-done
  6.4 1.8 %copy.8 = bf16[96,8,2,768]{3,1,2,0:T(8,128)(2,1)} copy(bf16[96,8,2,768]{3,2,1,0:T(2,128)(2,1)S(1)} %bitcast.5) | data formatting | bytes 4718592
  8.3 134.9 %by_head.1 = bf16[512,768]{1,0:T(8,128)(2,1)} custom-call(bf16[128,3072]{1,0:T(8,128)(2,1)} %modulate_part.1.hid_own, bf16[768,1536]{1,0:T(8,128)(2,1)} %bitcast.4, bf16[512,768]{1,0:T(8,128)(2,1)} %o_own.1, s32[8,128]{1,0:T(8,128)} %pad_add_fusion.lists, f32[1,768]{1,0:T(1,128)} %constant_dynamic-slice_fusion.gate), custom_call_target="tpu_custom_call" | custom-call | tf_op jit(solution)/shard_map/by_head/pallas_call | solution.py:704
  143.2 2.1 %copy.10 = bf16[512,768]{1,0:T(8,128)(2,1)} copy(bf16[512,768]{1,0:T(8,128)(2,1)} %by_head.1) | data formatting | bytes 1572864
Async XLA Ops:
  0.0 6.4 %copy-start = (bf16[768,2,768]{2,1,0:T(2,128)(2,1)S(1)}, bf16[768,2,768]{2,1,0:T(2,128)(2,1)}, u32[]{:S(2)}) copy-start(bf16[768,2,768]{2,1,0:T(2,128)(2,1)} %param.9) | copy-start | bytes 7077892
